TPU v7x, 512 devices: a whole 4x4x16 slice. The times are simulated.
512 devices in a mesh: grid: 64 (over y, z), member: 8 (over x, core).
Axes of the slice: x: 4, y: 4, z: 16, core: 2. Of those that a mesh axis runs over, the one named last changes fastest.
Arguments:
- state_ens: float32 [1024, 32, 128], P('grid', 'member'), may hold values from -6 to 6
- obs_ens: float32 [8192, 32, 128], P('grid', 'member'), may hold values from -6 to 6
- obs_value: float32 [8192, 128], P('grid'), may hold values from -8 to 8
- obs_rinv: float32 [8192, 128], P('grid'), may hold values from 0.25 to 4
- loc_weight: float32 [1024, 8, 8], P('grid'), may hold values from 0.05 to 1
- pair_block: int32 [1024, 8], P('grid'), may hold values from 0 to 383, as said below
- pair_count: int32 [1024], P('grid'), may hold values from 4 to 8, as said below
Outputs:
- analysis_ens: float32 [1024, 32, 128], P('grid', 'member')
Inputs may be any that keep to these rules, and one draw needn't show every extreme that they name: `pair_block`: pairs of a state block lie near its place within the slab, reaching into the neighbouring slabs; the first pair of every state block is in use. `pair_count`: the first state block of every slab uses all 8 pairs.
All inputs are finite; a program needn't handle non-finite values.
Results may differ from a plain program's by a relative error of at most 0.00017.
Values sent between devices are 32-bit elements; how exact they have to be, the bound alone decides.
No kernel may reach another device: no remote copies, remote signals or barrier semaphores. Data moves between devices by JAX's collectives and lax.ppermute only.
A program may use at most 64 MiB of HBM per device.

v0:
```python
import functools

import jax
import jax.numpy as jnp
from jax import lax
from jax.experimental import pallas as pl
from jax.experimental.pallas import tpu as pltpu
from jax.sharding import PartitionSpec as P

K = 32
BV = 128
Q = 8
P_SIZE = 8
NS = 7
SB = 16
OB = 128
MEMBERS = 8
GRID = 64
LANES = 128
F32 = jnp.float32
HIGHEST = lax.Precision.HIGHEST
INTERPRET = False
VMEM_BYTES = 8 << 20


def iota(shape, dim):
    return lax.broadcasted_iota(jnp.int32, shape, dim)


def slot_mask(row, column):
    return column == jnp.bitwise_and(row + 8, K - 1)


def call(kernel, out_rows, *args, smem=()):
    specs = [
        pl.BlockSpec(memory_space=pltpu.SMEM if i in smem else pltpu.VMEM)
        for i in range(len(args))
    ]
    return pl.pallas_call(
        kernel,
        out_shape=jax.ShapeDtypeStruct((out_rows, LANES), F32),
        in_specs=specs,
        out_specs=pl.BlockSpec(memory_space=pltpu.VMEM),
        compiler_params=pltpu.CompilerParams(vmem_limit_bytes=VMEM_BYTES),
        interpret=INTERPRET,
        name=kernel.__name__,
    )(*args)


def terms_kernel(member_ref, ens_ref, value_ref, rinv_ref, out_ref):
    start = pl.multiple_of(member_ref[0] * 16, 16)
    values = value_ref[pl.ds(start, 16), :]
    weights = rinv_ref[pl.ds(start, 16), :]
    part = iota((8, LANES), 1) // K
    column = jnp.bitwise_and(iota((8, LANES), 1), K - 1)
    slot = slot_mask(part * 8 + iota((8, LANES), 0), column)
    for row in range(16):
        tiles = [ens_ref[pl.ds(row * 4 + kk, 8, stride=64), :] for kk in range(4)]
        ensemble = jnp.concatenate(tiles, axis=0)
        mean = jnp.sum(ensemble, axis=0, keepdims=True) * (1.0 / K)
        perturb = ensemble - mean
        innovation = values[row : row + 1, :] - mean
        weighted = perturb * weights[row : row + 1, :]
        gram = lax.dot_general(
            weighted,
            jnp.concatenate([perturb] * 4, axis=0),
            (((1,), (1,)), ((), ())),
            precision=HIGHEST,
            preferred_element_type=F32,
        )
        vector = jnp.sum(weighted * innovation, axis=1, keepdims=True)
        terms = gram[0:8]
        vecs = jnp.broadcast_to(vector[0:8], (8, LANES))
        for kk in range(1, 4):
            here = part == kk
            terms = jnp.where(here, gram[kk * 8 : kk * 8 + 8], terms)
            vecs = jnp.where(here, vector[kk * 8 : kk * 8 + 8], vecs)
        out_ref[pl.ds(row, 8, stride=16), :] = jnp.where(slot, vecs, terms)


def window_kernel(in_ref, out_ref):
    for jb in range(2):
        rows = in_ref[pl.ds(jb, GRID, stride=2), :]
        out_ref[pl.ds(2 + jb, GRID, stride=6), :] = rows
        out_ref[pl.ds(jb, GRID, stride=6), :] = pltpu.roll(rows, 1, 0)
        out_ref[pl.ds(4 + jb, GRID, stride=6), :] = pltpu.roll(rows, GRID - 1, 0)


def combine_kernel(grid_ref, in_ref, weight_ref, block_ref, count_ref, state_ref, out_ref, combo_ref):
    slab = grid_ref[0]
    row = iota((6 * GRID, 1), 0)
    where = row // 6
    block = (row - where * 6) * GRID + where
    target = slab * OB + block - OB
    inside = jnp.logical_and(target >= 0, target < GRID * OB)
    block = jnp.where(inside, block, -1)
    picked = jnp.concatenate([block_ref[...]] * Q, axis=1)
    weight = jnp.concatenate([weight_ref[q] for q in range(Q)], axis=1)
    count = jnp.concatenate([count_ref[...]] * Q, axis=1)
    live = iota((P_SIZE, LANES), 0) < count
    weight = jnp.where(live, weight, 0.0)
    mix = jnp.zeros((6 * GRID, LANES), F32)
    for p in range(P_SIZE):
        mix = mix + jnp.where(block == picked[p : p + 1], weight[p : p + 1], 0.0)
    combo_ref[...] = lax.dot_general(
        mix,
        in_ref[...],
        (((0,), (0,)), ((), ())),
        precision=HIGHEST,
        preferred_element_type=F32,
    )
    for q in range(Q):
        for s0 in range(2):
            out_ref[pl.ds(q * 2 + s0, 8, stride=24), :] = combo_ref[pl.ds(q * 16 + s0, 8, stride=2), :]
    for r in range(8):
        out_ref[pl.ds(16 + r, 8, stride=24), :] = state_ref[pl.ds(r, 8, stride=8), :]


def spread(flat, mask):
    return jnp.where(mask, jnp.concatenate([flat] * 8, axis=0), 0.0)


def product(left, right):
    return jnp.dot(left, right, precision=HIGHEST, preferred_element_type=F32)


def transform_kernel(in_ref, out_ref):
    width = Q * K
    mask = iota((width, width), 0) // K == iota((width, width), 1) // K
    ones = mask.astype(F32)
    part = iota((8, LANES), 1) // K
    row = iota((K, width), 0)
    column = jnp.bitwise_and(iota((K, width), 1), K - 1)
    slot = slot_mask(row, column)
    identity = (row == column).astype(F32)
    slab_v = iota((K, LANES), 1) // (BV // Q)
    for s0 in range(2):
        tiles = [in_ref[pl.ds(q * 2 + s0, 8, stride=24), :] for q in range(Q)]
        rows = []
        for kk in range(4):
            halves = []
            for half in range(2):
                acc = None
                for qq in range(4):
                    tile = tiles[half * 4 + qq]
                    shift = (qq - kk) * K % LANES
                    if shift:
                        tile = pltpu.roll(tile, shift, 1)
                    acc = tile if acc is None else jnp.where(part == qq, tile, acc)
                halves.append(acc)
            rows.append(jnp.concatenate(halves, axis=1))
        packed = jnp.concatenate(rows, axis=0)
        lifted = jnp.concatenate([packed[8:], packed[:8]], axis=0)
        mirror = jnp.where(
            column >= 8, pltpu.roll(lifted, 8, 1), pltpu.roll(lifted, width - 24, 1)
        )
        amat = jnp.where(slot, mirror, packed) + (K - 1.0) * identity
        squares = jnp.sum(amat * amat, axis=0, keepdims=True)
        sums = product(
            jnp.concatenate(
                [jnp.where(slot, packed, 0.0), jnp.broadcast_to(squares, (8, width))], axis=0
            ),
            ones,
        )
        drive = sums[:K]
        frobenius = jnp.sqrt(sums[K : K + 1])
        root = amat / frobenius
        middle = 1.5 * identity - 0.5 * root
        both = product(root, spread(middle, mask))
        root = both
        inverse = middle
        for _ in range(1, NS - 1):
            middle = 1.5 * identity - 0.5 * product(inverse, spread(root, mask))
            both = product(jnp.concatenate([root, inverse], axis=0), spread(middle, mask))
            root = both[:K]
            inverse = both[K:]
        middle = 1.5 * identity - 0.5 * product(inverse, spread(root, mask))
        inverse = product(inverse, spread(middle, mask))
        first = jnp.sum(inverse * drive, axis=0, keepdims=True)
        wmean = product(inverse * first, ones) / frobenius
        trans = jnp.sqrt(K - 1.0) * inverse / jnp.sqrt(frobenius) + wmean
        state = jnp.concatenate(
            [in_ref[pl.ds(16 + s0 * 4 + kk, 8, stride=24), :] for kk in range(4)], axis=0
        )
        full = lax.dot_general(
            trans,
            state,
            (((0,), (0,)), ((), ())),
            precision=HIGHEST,
            preferred_element_type=F32,
        )
        update = full[0:K]
        for q in range(1, Q):
            update = jnp.where(slab_v == q, full[q * K : (q + 1) * K], update)
        for kk in range(4):
            out_ref[pl.ds(s0 * 4 + kk, 8, stride=8), :] = update[kk * 8 : kk * 8 + 8]


def swap(array, axis):
    return lax.all_to_all(array, axis, split_axis=0, concat_axis=0, tiled=True)


def local(state_ens, obs_ens, obs_value, obs_rinv, loc_weight, pair_block, pair_count):
    member = lax.axis_index("member").astype(jnp.int32).reshape(1)
    slab = lax.axis_index("grid").astype(jnp.int32).reshape(1)
    gathered = swap(obs_ens.reshape(OB * 4, LANES), "member")
    terms = call(terms_kernel, OB, member, gathered, obs_value, obs_rinv, smem=(0,))
    shares = swap(terms, "member")
    windows = call(window_kernel, 6 * GRID, shares)
    arrived = swap(windows.reshape(3 * GRID, 2, LANES), "grid").reshape(6 * GRID, LANES)
    combos = pl.pallas_call(
        combine_kernel,
        out_shape=jax.ShapeDtypeStruct((8 * 24, LANES), F32),
        in_specs=[pl.BlockSpec(memory_space=pltpu.SMEM)] + [pl.BlockSpec(memory_space=pltpu.VMEM)] * 5,
        out_specs=pl.BlockSpec(memory_space=pltpu.VMEM),
        scratch_shapes=[pltpu.VMEM((LANES, LANES), F32)],
        compiler_params=pltpu.CompilerParams(vmem_limit_bytes=VMEM_BYTES),
        interpret=INTERPRET,
        name="combine_kernel",
    )(
        slab,
        arrived,
        jnp.transpose(loc_weight, (1, 2, 0)),
        jnp.transpose(pair_block, (1, 0)),
        pair_count.reshape(1, SB),
        state_ens.reshape(SB * 4, LANES),
    )
    matrices = swap(combos, "member")
    update = call(transform_kernel, SB * 4, matrices)
    return swap(update, "member").reshape(SB, 4, BV)


def solution(mesh):
    return jax.shard_map(
        local,
        mesh=mesh,
        in_specs=(
            P("grid", "member", None),
            P("grid", "member", None),
            P("grid", None),
            P("grid", None),
            P("grid", None, None),
            P("grid", None),
            P("grid"),
        ),
        out_specs=P("grid", "member", None),
        check_vma=False,
    )
```

profile of v0, /device:TPU:1, one launch (start us, length us, event | category | flops | bytes accessed | tf_op | source)
XLA Modules:
  0.0 88.8 jit_solution(6739082314013391680)
XLA Ops:
  0.0 0.0 copy-start
  0.0 0.0 copy-start.1
  0.0 10.3 %all-to-all-start = ((f32[8,64,128]{2,1,0:T(8,128)}), f32[8,64,128]{2,1,0:T(8,128)S(1)}, u32[]{:S(2)}, u32[]{:S(2)}) async-start(f32[8,64,128]{2,1,0:T(8,128)} %bitcast.27), calls=%async_computation | async-start | bytes 524288 | tf_op jit(solution)/shard_map/all_to_all | solution.py:200
  10.3 6.5 %all-to-all-done = f32[8,64,128]{2,1,0:T(8,128)S(1)} async-done(((f32[8,64,128]{2,1,0:T(8,128)}), f32[8,64,128]{2,1,0:T(8,128)S(1)}, u32[]{:S(2)}, u32[]{:S(2)}) %all-to-all-start) | async-done | bytes 262176 | tf_op jit(solution)/shard_map/all_to_all | solution.py:200
  16.8 0.0 copy-done
  16.8 0.0 copy-done.1
  16.8 1.8 %terms_kernel.1 = f32[128,128]{1,0:T(8,128)S(1)} custom-call(s32[1]{0:T(128)} %bitcast.1.member_ref, f32[512,128]{1,0:T(8,128)S(1)} %bitcast.16, f32[128,128]{1,0:T(8,128)S(1)} %copy-done, f32[128,128]{1,0:T(8,128)S(1)} %copy-done.1), custom_call_target="tpu_custom_call" | custom-call | tf_op jit(solution)/shard_map/terms_kernel/pallas_call | solution.py:39
  18.6 8.3 %all_to_all.47 = f32[8,16,128]{2,1,0:T(8,128)S(1)} all-to-all(f32[8,16,128]{2,1,0:T(8,128)S(1)} %bitcast.20), channel_id=1, replica_groups=mesh['grid'=64,'member'=8] {'member'}, dimensions={0} | all-to-all | bytes 131072 | tf_op jit(solution)/shard_map/all_to_all | solution.py:200
  26.8 0.7 window_kernel.1
  27.5 0.0 copy-start.2
  27.5 0.0 copy-start.3
  27.5 14.2 %all-to-all-start.2 = ((f32[192,2,128]{2,1,0:T(2,128)}), f32[192,2,128]{2,1,0:T(2,128)S(1)}, u32[]{:S(2)}, u32[]{:S(2)}) async-start(f32[192,2,128]{2,1,0:T(2,128)} %bitcast.6), calls=%async_computation.2 | async-start | bytes 393216 | tf_op jit(solution)/shard_map/all_to_all | solution.py:200
  41.7 16.3 %all-to-all-done.2 = f32[192,2,128]{2,1,0:T(2,128)S(1)} async-done(((f32[192,2,128]{2,1,0:T(2,128)}), f32[192,2,128]{2,1,0:T(2,128)S(1)}, u32[]{:S(2)}, u32[]{:S(2)}) %all-to-all-start.2) | async-done | bytes 196640 | tf_op jit(solution)/shard_map/all_to_all | solution.py:200
  58.0 0.0 copy-start.4
  58.0 0.0 copy-start.5
  58.0 0.0 copy-done.2
  58.0 0.0 copy-done.3
  58.0 0.7 copy-done.4
  58.7 0.0 copy-done.5
  58.7 0.6 combine_kernel.1
  59.3 10.2 %all_to_all.48 = f32[8,24,128]{2,1,0:T(8,128)S(1)} all-to-all(f32[8,24,128]{2,1,0:T(8,128)S(1)} %bitcast.19), channel_id=1, replica_groups=mesh['grid'=64,'member'=8] {'member'}, dimensions={0} | all-to-all | bytes 196608 | tf_op jit(solution)/shard_map/all_to_all | solution.py:200
  69.6 10.7 %transform_kernel.1 = f32[64,128]{1,0:T(8,128)S(1)} custom-call(f32[192,128]{1,0:T(8,128)S(1)} %bitcast.18), custom_call_target="tpu_custom_call" | custom-call | tf_op jit(solution)/shard_map/transform_kernel/pallas_call | solution.py:39
  80.3 7.9 %all_to_all.49 = f32[8,8,128]{2,1,0:T(8,128)S(1)} all-to-all(f32[8,8,128]{2,1,0:T(8,128)S(1)} %bitcast.22), channel_id=1, replica_groups=mesh['grid'=64,'member'=8] {'member'}, dimensions={0} | all-to-all | bytes 65536 | tf_op jit(solution)/shard_map/all_to_all | solution.py:200
  88.2 0.6 copy.9
Async XLA Ops:
  0.0 16.8 %copy-start = (f32[128,128]{1,0:T(8,128)S(1)}, f32[128,128]{1,0:T(8,128)}, u32[]{:S(2)}) copy-start(f32[128,128]{1,0:T(8,128)} %value_ref.1) | copy-start | bytes 196612
  0.0 16.8 %copy-start.1 = (f32[128,128]{1,0:T(8,128)S(1)}, f32[128,128]{1,0:T(8,128)}, u32[]{:S(2)}) copy-start(f32[128,128]{1,0:T(8,128)} %rinv_ref.1) | copy-start | bytes 196612
  0.0 16.8 %all-to-all-start = ((f32[8,64,128]{2,1,0:T(8,128)}), f32[8,64,128]{2,1,0:T(8,128)S(1)}, u32[]{:S(2)}, u32[]{:S(2)}) async-start(f32[8,64,128]{2,1,0:T(8,128)} %bitcast.27), calls=%async_computation | async-start | bytes 524288 | tf_op jit(solution)/shard_map/all_to_all | solution.py:200
  27.5 30.5 %copy-start.2 = (f32[16,8,8]{0,2,1:T(8,128)S(1)}, f32[16,8,8]{0,2,1:T(8,128)}, u32[]{:S(2)}) copy-start(f32[16,8,8]{0,2,1:T(8,128)} %param.11) | copy-start | bytes 12292
  27.5 30.5 %copy-start.3 = (f32[16,4,128]{2,1,0:T(4,128)S(1)}, f32[16,4,128]{2,1,0:T(4,128)}, u32[]{:S(2)}) copy-start(f32[16,4,128]{2,1,0:T(4,128)} %param.7) | copy-start | bytes 98308
  27.5 30.5 %all-to-all-start.2 = ((f32[192,2,128]{2,1,0:T(2,128)}), f32[192,2,128]{2,1,0:T(2,128)S(1)}, u32[]{:S(2)}, u32[]{:S(2)}) async-start(f32[192,2,128]{2,1,0:T(2,128)} %bitcast.6), calls=%async_computation.2 | async-start | bytes 393216 | tf_op jit(solution)/shard_map/all_to_all | solution.py:200
  58.0 0.7 copy-start.4
  58.0 0.7 copy-start.5
where the time goes:
time: 89.3 us; the launch traced here: 88.8 us
  blocking collectives  26.4 us (30%)
  starting transfers between devices  24.5 us (27%)
  waiting for transfers between devices  22.8 us (26%)
  Pallas kernels  13.8 us (15%)
  local copies, waits for them, and re-layouts  1.31 us (1%)
    all_to_all x3, blocking collectives, swap(): return lax.all_to_all(array, axis, split_axis=0, concat_axis=0, tiled=True)  26.4 us
    all_to_all x2, starting transfers between devices, swap(): return lax.all_to_all(array, axis, split_axis=0, concat_axis=0, tiled=True)  24.5 us
    all_to_all x2, waiting for transfers between devices, swap(): return lax.all_to_all(array, axis, split_axis=0, concat_axis=0, tiled=True)  22.8 us
    pallas_call x3, Pallas kernels, call(): pl.pallas_call(kernel, out_shape=jax.ShapeDtypeStruct((out_rows, LANES),...  13.2 us
  transfers between devices with their start and end apart: 2, of which 2 were waited for; matrix products, arithmetic and copies ran while one was open for 0% of the time, Pallas kernels for 0%

commit v1 on v0

v1 whole, which is shorter than its diff:
```python
import functools

import jax
import jax.numpy as jnp
from jax import lax
from jax.experimental import pallas as pl
from jax.experimental.pallas import tpu as pltpu
from jax.sharding import PartitionSpec as P

K = 32
BV = 128
Q = 8
P_SIZE = 8
NS = 7
SB = 16
OB = 128
MEMBERS = 8
GRID = 64
LANES = 128
F32 = jnp.float32
BF16 = jnp.bfloat16
HIGHEST = lax.Precision.HIGHEST
INTERPRET = False
VMEM_BYTES = 8 << 20


def iota(shape, dim):
    return lax.broadcasted_iota(jnp.int32, shape, dim)


def slot_mask(row, column):
    return column == jnp.bitwise_and(row + 8, K - 1)


def call(kernel, out_rows, *args, scalars=0, unplaced=0, scratch=()):
    vmem = pl.BlockSpec(memory_space=pltpu.VMEM)
    placed = [vmem] * (len(args) - scalars - unplaced)
    return pl.pallas_call(
        kernel,
        out_shape=[jax.ShapeDtypeStruct((rows, LANES), F32) for rows in out_rows],
        in_specs=[pl.BlockSpec(memory_space=pltpu.SMEM)] * scalars
        + placed
        + [pl.BlockSpec(memory_space=pltpu.HBM)] * unplaced,
        out_specs=[vmem] * len(out_rows),
        scratch_shapes=scratch,
        compiler_params=pltpu.CompilerParams(vmem_limit_bytes=VMEM_BYTES),
        interpret=INTERPRET,
        name=kernel.__name__,
    )(*args)


def hold(array):
    return array if INTERPRET else pltpu.with_memory_space_constraint(array, pltpu.HBM)


def mixing(slab, weight_ref, block_ref, count_ref):
    row = iota((6 * GRID, 1), 0)
    where = row // 6
    block = (row - where * 6) * GRID + where
    target = slab * OB + block - OB
    inside = jnp.logical_and(target >= 0, target < GRID * OB)
    block = jnp.where(inside, block, -1)
    picked = jnp.concatenate([block_ref[...]] * Q, axis=1)
    weight = jnp.concatenate([weight_ref[q] for q in range(Q)], axis=1)
    count = jnp.concatenate([count_ref[...]] * Q, axis=1)
    live = iota((P_SIZE, LANES), 0) < count
    weight = jnp.where(live, weight, 0.0)
    mix = jnp.zeros((6 * GRID, LANES), F32)
    for p in range(P_SIZE):
        mix = mix + jnp.where(block == picked[p : p + 1], weight[p : p + 1], 0.0)
    return mix


def terms_kernel(
    slab_ref,
    member_ref,
    ens_ref,
    value_ref,
    rinv_ref,
    weight_ref,
    block_hbm,
    count_hbm,
    out_ref,
    mix_ref,
    block_ref,
    count_ref,
    sems,
):
    fetches = [
        pltpu.make_async_copy(block_hbm, block_ref, sems.at[0]),
        pltpu.make_async_copy(count_hbm, count_ref, sems.at[1]),
    ]
    for fetch in fetches:
        fetch.start()
    start = pl.multiple_of(member_ref[0] * 16, 16)
    values = value_ref[pl.ds(start, 16), :]
    weights = rinv_ref[pl.ds(start, 16), :]
    part = iota((8, LANES), 1) // K
    column = jnp.bitwise_and(iota((8, LANES), 1), K - 1)
    slot = slot_mask(part * 8 + iota((8, LANES), 0), column)
    for row in range(16):
        tiles = [ens_ref[pl.ds(row * 4 + kk, 8, stride=64), :] for kk in range(4)]
        ensemble = jnp.concatenate(tiles, axis=0)
        mean = jnp.sum(ensemble, axis=0, keepdims=True) * (1.0 / K)
        perturb = ensemble - mean
        innovation = values[row : row + 1, :] - mean
        weighted = perturb * weights[row : row + 1, :]
        gram = lax.dot_general(
            weighted,
            jnp.concatenate([perturb] * 4, axis=0),
            (((1,), (1,)), ((), ())),
            precision=HIGHEST,
            preferred_element_type=F32,
        )
        vector = jnp.sum(weighted * innovation, axis=1, keepdims=True)
        terms = gram[0:8]
        vecs = jnp.broadcast_to(vector[0:8], (8, LANES))
        for kk in range(1, 4):
            here = part == kk
            terms = jnp.where(here, gram[kk * 8 : kk * 8 + 8], terms)
            vecs = jnp.where(here, vector[kk * 8 : kk * 8 + 8], vecs)
        out_ref[pl.ds(row, 8, stride=16), :] = jnp.where(slot, vecs, terms)
    for fetch in fetches:
        fetch.wait()
    mix_ref[...] = mixing(slab_ref[0], weight_ref, block_ref, count_ref)


def window_kernel(in_ref, out_ref):
    for jb in range(2):
        rows = in_ref[pl.ds(jb, GRID, stride=2), :]
        out_ref[pl.ds(2 + jb, GRID, stride=6), :] = rows
        out_ref[pl.ds(jb, GRID, stride=6), :] = pltpu.roll(rows, 1, 0)
        out_ref[pl.ds(4 + jb, GRID, stride=6), :] = pltpu.roll(rows, GRID - 1, 0)


def combine_kernel(in_ref, mix_ref, state_ref, out_ref, combo_ref):
    combo_ref[...] = lax.dot_general(
        mix_ref[...],
        in_ref[...],
        (((0,), (0,)), ((), ())),
        precision=HIGHEST,
        preferred_element_type=F32,
    )
    for q in range(Q):
        for s0 in range(2):
            out_ref[pl.ds(q * 2 + s0, 8, stride=24), :] = combo_ref[pl.ds(q * 16 + s0, 8, stride=2), :]
    for r in range(8):
        out_ref[pl.ds(16 + r, 8, stride=24), :] = state_ref[pl.ds(r, 8, stride=8), :]


def halves(value):
    high = value.astype(BF16)
    return high, (value - high.astype(F32)).astype(BF16)


def dot(left, right):
    return jnp.dot(left, right, preferred_element_type=F32)


def product(left, right, ones):
    high, low = halves(left)
    right_high, right_low = (jnp.concatenate([half] * Q, axis=0) * ones for half in halves(right))
    rows = left.shape[0]
    wide = dot(jnp.concatenate([high, low], axis=0), right_high)
    return wide[:rows] + wide[rows:] + dot(high, right_low)


def segment_sum(value, ones):
    high, rest = value.astype(BF16), value
    rest = rest - high.astype(F32)
    middle = rest.astype(BF16)
    low = (rest - middle.astype(F32)).astype(BF16)
    rows = value.shape[0]
    wide = dot(jnp.concatenate([high, middle, low], axis=0), ones)
    return wide[:rows] + wide[rows : 2 * rows] + wide[2 * rows :]


def roll_segment(value, shift, column):
    width = value.shape[1]
    return jnp.where(
        column >= shift, pltpu.roll(value, shift, 1), pltpu.roll(value, width - K + shift, 1)
    )


def transform_kernel(in_ref, out_ref):
    width = Q * K
    ones = (iota((width, width), 0) // K == iota((width, width), 1) // K).astype(F32).astype(BF16)
    part = iota((8, LANES), 1) // K
    row = iota((K, width), 0)
    column = jnp.bitwise_and(iota((K, width), 1), K - 1)
    slot = slot_mask(row, column)
    identity = (row == column).astype(F32)
    point = iota((width, BV), 0) // K == iota((width, BV), 1) // (BV // Q)
    point = point.astype(F32).astype(BF16)
    pair = range(2)
    amats, drives = [], []
    for s0 in pair:
        tiles = [in_ref[pl.ds(q * 2 + s0, 8, stride=24), :] for q in range(Q)]
        rows = []
        for kk in range(4):
            sides = []
            for half in range(2):
                acc = None
                for qq in range(4):
                    tile = tiles[half * 4 + qq]
                    shift = (qq - kk) * K % LANES
                    if shift:
                        tile = pltpu.roll(tile, shift, 1)
                    acc = tile if acc is None else jnp.where(part == qq, tile, acc)
                sides.append(acc)
            rows.append(jnp.concatenate(sides, axis=1))
        packed = jnp.concatenate(rows, axis=0)
        mirror = roll_segment(jnp.concatenate(rows[1:] + rows[:1], axis=0), 8, column)
        amats.append(jnp.where(slot, mirror, packed) + (K - 1.0) * identity)
        drive = jnp.sum(jnp.where(slot, packed, 0.0), axis=0, keepdims=True)
        drives.append(roll_segment(jnp.broadcast_to(drive, (8, width)), K - 8, column[:8])[:1])
    squares = [
        jnp.broadcast_to(jnp.sum(amat * amat, axis=0, keepdims=True), (8, width)) for amat in amats
    ]
    sums = segment_sum(jnp.concatenate(squares, axis=0), ones)
    frobenius = [jnp.sqrt(sums[8 * s0 : 8 * s0 + 1]) for s0 in pair]
    root = [amats[s0] / frobenius[s0] for s0 in pair]
    inverse = [1.5 * identity - 0.5 * root[s0] for s0 in pair]
    root = [product(root[s0], inverse[s0], ones) for s0 in pair]
    for _ in range(1, NS - 1):
        middle = [1.5 * identity - 0.5 * product(inverse[s0], root[s0], ones) for s0 in pair]
        both = [
            product(jnp.concatenate([root[s0], inverse[s0]], axis=0), middle[s0], ones) for s0 in pair
        ]
        root = [both[s0][:K] for s0 in pair]
        inverse = [both[s0][K:] for s0 in pair]
    middle = [1.5 * identity - 0.5 * product(inverse[s0], root[s0], ones) for s0 in pair]
    inverse = [product(inverse[s0], middle[s0], ones) for s0 in pair]
    first = [segment_sum(inverse[s0] * drives[s0], ones) for s0 in pair]
    for s0 in pair:
        wmean = jnp.sum(inverse[s0] * first[s0], axis=0, keepdims=True) / frobenius[s0]
        trans = inverse[s0] * (jnp.sqrt(K - 1.0) / jnp.sqrt(frobenius[s0])) + wmean
        state = jnp.concatenate(
            [in_ref[pl.ds(16 + s0 * 4 + kk, 8, stride=24), :] for kk in range(4)], axis=0
        )
        update = product(trans, state, point)
        for kk in range(4):
            out_ref[pl.ds(s0 * 4 + kk, 8, stride=8), :] = update[kk * 8 : kk * 8 + 8]


def swap(array, axis):
    return lax.all_to_all(array, axis, split_axis=0, concat_axis=0, tiled=True)


def local(state_ens, obs_ens, obs_value, obs_rinv, loc_weight, pair_block, pair_count):
    slab = lax.axis_index("grid").astype(jnp.int32).reshape(1)
    member = lax.axis_index("member").astype(jnp.int32).reshape(1)
    gathered = swap(obs_ens.reshape(OB * 4, LANES), "member")
    terms, mix = call(
        terms_kernel,
        (OB, 6 * GRID),
        slab,
        member,
        gathered,
        obs_value,
        obs_rinv,
        jnp.transpose(loc_weight, (1, 2, 0)),
        hold(jnp.transpose(pair_block, (1, 0))),
        hold(pair_count.reshape(1, SB)),
        scalars=2,
        unplaced=2,
        scratch=[
            pltpu.VMEM((P_SIZE, SB), jnp.int32),
            pltpu.VMEM((1, SB), jnp.int32),
            pltpu.SemaphoreType.DMA((2,)),
        ],
    )
    shares = swap(terms, "member")
    (windows,) = call(window_kernel, (6 * GRID,), shares)
    arrived = swap(windows.reshape(3 * GRID, 2, LANES), "grid").reshape(6 * GRID, LANES)
    (combos,) = call(
        combine_kernel,
        (8 * 24,),
        arrived,
        mix,
        state_ens.reshape(SB * 4, LANES),
        scratch=[pltpu.VMEM((LANES, LANES), F32)],
    )
    matrices = swap(combos, "member")
    (update,) = call(transform_kernel, (SB * 4,), matrices)
    return swap(update.reshape(SB, 4, BV), "member")


def solution(mesh):
    return jax.shard_map(
        local,
        mesh=mesh,
        in_specs=(
            P("grid", "member", None),
            P("grid", "member", None),
            P("grid", None),
            P("grid", None),
            P("grid", None, None),
            P("grid", None),
            P("grid"),
        ),
        out_specs=P("grid", "member", None),
        check_vma=False,
    )
```

time: 89.3 us -> 80.3 us (0.90)
  blocking collectives: 26.4 us -> 56.6 us
  waiting for transfers between devices: 22.8 us -> 6.5 us
  starting transfers between devices: 24.5 us -> 10.3 us
  Pallas kernels: 13.8 us -> 5.9 us
    all_to_all x3 -> x4, blocking collectives: 26.4 us -> 56.6 us  [swap(): return lax.all_to_all(array, axis, split_axis=0, concat_axis=0, tiled=True)]
    all_to_all x2 -> x1, waiting for transfers between devices: 22.8 us -> 6.5 us  [swap(): return lax.all_to_all(array, axis, split_axis=0, concat_axis=0, tiled=True)]
    all_to_all x2 -> x1, starting transfers between devices: 24.5 us -> 10.3 us  [swap(): return lax.all_to_all(array, axis, split_axis=0, concat_axis=0, tiled=True)]
    pallas_call x4, Pallas kernels: 13.8 us -> 5.9 us  [call(): pl.pallas_call(kernel, out_shape=[jax.ShapeDtypeStruct((rows, LANES), F32...]
  transfers between devices with their start and end apart: 2 -> 1, of which waited for: 2 -> 1; matrix products, arithmetic and copies ran while one was open for 0% -> 0% of each run, Pallas kernels for 0% -> 0%
where the time goes in v1:
time: 80.3 us; the launch traced here: 79.9 us
  blocking collectives  56.6 us (70%)
  starting transfers between devices  10.3 us (13%)
  waiting for transfers between devices  6.5 us (8%)
  Pallas kernels  5.9 us (7%)
    all_to_all x4, blocking collectives, swap(): return lax.all_to_all(array, axis, split_axis=0, concat_axis=0, tiled=True)  56.6 us
    all_to_all x1, starting transfers between devices, swap(): return lax.all_to_all(array, axis, split_axis=0, concat_axis=0, tiled=True)  10.3 us
    all_to_all x1, waiting for transfers between devices, swap(): return lax.all_to_all(array, axis, split_axis=0, concat_axis=0, tiled=True)  6.5 us
    pallas_call x4, Pallas kernels, call(): pl.pallas_call(kernel, out_shape=[jax.ShapeDtypeStruct((rows, LANES), F32...  5.9 us
  transfers between devices with their start and end apart: 1, of which 1 were waited for; matrix products, arithmetic and copies ran while one was open for 0% of the time, Pallas kernels for 0%

profile of v1, /device:TPU:1, one launch (start us, length us, event | category | flops | bytes accessed | tf_op | source)
XLA Modules:
  0.0 79.9 jit_solution(528240984094090659)
XLA Ops:
  0.0 0.0 copy-start
  0.0 0.0 copy-start.1
  0.0 0.0 copy-start.3
  0.0 10.3 %all-to-all-start = ((f32[8,64,128]{2,1,0:T(8,128)}), f32[8,64,128]{2,1,0:T(8,128)S(1)}, u32[]{:S(2)}, u32[]{:S(2)}) async-start(f32[8,64,128]{2,1,0:T(8,128)} %bitcast.25), calls=%async_computation | async-start | bytes 524288 | tf_op jit(solution)/shard_map/all_to_all | solution.py:247
  10.3 6.5 %all-to-all-done = f32[8,64,128]{2,1,0:T(8,128)S(1)} async-done(((f32[8,64,128]{2,1,0:T(8,128)}), f32[8,64,128]{2,1,0:T(8,128)S(1)}, u32[]{:S(2)}, u32[]{:S(2)}) %all-to-all-start) | async-done | bytes 262176 | tf_op jit(solution)/shard_map/all_to_all | solution.py:247
  16.8 0.0 copy-done
  16.8 0.0 copy-done.1
  16.8 0.0 copy-done.3
  16.8 2.2 %terms_kernel.1 = (f32[128,128]{1,0:T(8,128)S(1)}, f32[384,128]{1,0:T(8,128)S(1)}) custom-call(s32[1]{0:T(128)} %bitcast.slab_ref, s32[1]{0:T(128)} %bitcast.1.member_ref, f32[512,128]{1,0:T(8,128)S(1)} %bitcast.15, f32[128,128]{1,0:T(8,128)S(1)} %copy-done, f32[128,128]{1,0:T(8,128)S(1)} %copy-done.1, f32[8,8,16]{2,1,0:T(8,128)S(1)} %bitcast.24, ...), custom_call_target="tpu_custom_call" | custom-call | tf_op jit(solution)/shard_map/terms_kernel/pallas_call | solution.py:38
  19.0 8.3 %all_to_all.43 = f32[8,16,128]{2,1,0:T(8,128)S(1)} all-to-all(f32[8,16,128]{2,1,0:T(8,128)S(1)} %bitcast.22), channel_id=1, replica_groups=mesh['grid'=64,'member'=8] {'member'}, dimensions={0} | all-to-all | bytes 131072 | tf_op jit(solution)/shard_map/all_to_all | solution.py:247
  27.3 0.0 copy-start.2
  27.3 30.2 %all_to_all.44 = f32[192,2,128]{2,1,0:T(2,128)S(1)} all-to-all(f32[192,2,128]{2,1,0:T(2,128)S(1)} %bitcast.16), channel_id=1, replica_groups=mesh['grid'=64,'member'=8] {'grid'}, dimensions={0} | all-to-all | bytes 393216 | tf_op jit(solution)/shard_map/all_to_all | solution.py:247
  57.5 0.0 copy-done.2
  57.5 0.4 combine_kernel.1
  57.8 10.2 %all_to_all.45 = f32[8,24,128]{2,1,0:T(8,128)S(1)} all-to-all(f32[8,24,128]{2,1,0:T(8,128)S(1)} %bitcast.18), channel_id=1, replica_groups=mesh['grid'=64,'member'=8] {'member'}, dimensions={0} | all-to-all | bytes 196608 | tf_op jit(solution)/shard_map/all_to_all | solution.py:247
  68.1 3.3 %transform_kernel.1 = f32[64,128]{1,0:T(8,128)S(1)} custom-call(f32[192,128]{1,0:T(8,128)S(1)} %bitcast.19), custom_call_target="tpu_custom_call" | custom-call | tf_op jit(solution)/shard_map/transform_kernel/pallas_call | solution.py:38
  71.4 7.9 %all_to_all.46 = f32[16,4,128]{2,1,0:T(4,128)S(1)} all-to-all(f32[16,4,128]{2,1,0:T(4,128)S(1)} %bitcast.21), channel_id=1, replica_groups=mesh['grid'=64,'member'=8] {'member'}, dimensions={0} | all-to-all | bytes 65536 | tf_op jit(solution)/shard_map/all_to_all | solution.py:247
  79.3 0.6 copy.9
  (1 shorter events, 0.0 us)
Async XLA Ops:
  0.0 16.8 %copy-start = (f32[128,128]{1,0:T(8,128)S(1)}, f32[128,128]{1,0:T(8,128)}, u32[]{:S(2)}) copy-start(f32[128,128]{1,0:T(8,128)} %value_ref.1) | copy-start | bytes 196612
  0.0 16.8 %copy-start.1 = (f32[128,128]{1,0:T(8,128)S(1)}, f32[128,128]{1,0:T(8,128)}, u32[]{:S(2)}) copy-start(f32[128,128]{1,0:T(8,128)} %rinv_ref.1) | copy-start | bytes 196612
  0.0 16.8 %copy-start.3 = (f32[16,8,8]{0,2,1:T(8,128)S(1)}, f32[16,8,8]{0,2,1:T(8,128)}, u32[]{:S(2)}) copy-start(f32[16,8,8]{0,2,1:T(8,128)} %param.11) | copy-start | bytes 12292
  0.0 16.8 %all-to-all-start = ((f32[8,64,128]{2,1,0:T(8,128)}), f32[8,64,128]{2,1,0:T(8,128)S(1)}, u32[]{:S(2)}, u32[]{:S(2)}) async-start(f32[8,64,128]{2,1,0:T(8,128)} %bitcast.25), calls=%async_computation | async-start | bytes 524288 | tf_op jit(solution)/shard_map/all_to_all | solution.py:247
  27.3 30.2 %copy-start.2 = (f32[16,4,128]{2,1,0:T(4,128)S(1)}, f32[16,4,128]{2,1,0:T(4,128)}, u32[]{:S(2)}) copy-start(f32[16,4,128]{2,1,0:T(4,128)} %param.7) | copy-start | bytes 98308

commit v2 on v1

--- a/solution.py
+++ b/solution.py
@@ -23,13 +23,28 @@
 INTERPRET = False
 VMEM_BYTES = 8 << 20
 
+START = (0, 32, 56, 72)
+
 
 def iota(shape, dim):
     return lax.broadcasted_iota(jnp.int32, shape, dim)
 
 
-def slot_mask(row, column):
-    return column == jnp.bitwise_and(row + 8, K - 1)
+def low3(value):
+    return jnp.bitwise_and(value, 7)
+
+
+def halves(value):
+    high = value.astype(BF16)
+    return high, (value - high.astype(F32)).astype(BF16)
+
+
+def dot(left, right):
+    return jnp.dot(left, right, preferred_element_type=F32)
+
+
+def dot_rows(left, right):
+    return lax.dot_general(left, right, (((1,), (1,)), ((), ())), preferred_element_type=F32)
 
 
 def call(kernel, out_rows, *args, scalars=0, unplaced=0, scratch=()):
@@ -53,22 +68,21 @@
     return array if INTERPRET else pltpu.with_memory_space_constraint(array, pltpu.HBM)
 
 
-def mixing(slab, weight_ref, block_ref, count_ref):
-    row = iota((6 * GRID, 1), 0)
-    where = row // 6
-    block = (row - where * 6) * GRID + where
-    target = slab * OB + block - OB
-    inside = jnp.logical_and(target >= 0, target < GRID * OB)
-    block = jnp.where(inside, block, -1)
+def mixing(slab, weight_ref, block_ref, count_ref, mix_ref):
     picked = jnp.concatenate([block_ref[...]] * Q, axis=1)
     weight = jnp.concatenate([weight_ref[q] for q in range(Q)], axis=1)
     count = jnp.concatenate([count_ref[...]] * Q, axis=1)
-    live = iota((P_SIZE, LANES), 0) < count
-    weight = jnp.where(live, weight, 0.0)
-    mix = jnp.zeros((6 * GRID, LANES), F32)
-    for p in range(P_SIZE):
-        mix = mix + jnp.where(block == picked[p : p + 1], weight[p : p + 1], 0.0)
-    return mix
+    target = slab * OB + picked - OB
+    used = jnp.logical_and(target >= 0, target < GRID * OB)
+    used = jnp.logical_and(used, iota((P_SIZE, LANES), 0) < count)
+    weight = jnp.where(used, weight, 0.0)
+    step = 16
+    block = iota((step, LANES), 0)
+    for first in range(0, 3 * OB, step):
+        mix = jnp.zeros((step, LANES), F32)
+        for p in range(P_SIZE):
+            mix = mix + jnp.where(block + first == picked[p : p + 1], weight[p : p + 1], 0.0)
+        mix_ref[first : first + step] = mix
 
 
 def terms_kernel(
@@ -95,48 +109,78 @@
     start = pl.multiple_of(member_ref[0] * 16, 16)
     values = value_ref[pl.ds(start, 16), :]
     weights = rinv_ref[pl.ds(start, 16), :]
-    part = iota((8, LANES), 1) // K
-    column = jnp.bitwise_and(iota((8, LANES), 1), K - 1)
-    slot = slot_mask(part * 8 + iota((8, LANES), 0), column)
-    for row in range(16):
-        tiles = [ens_ref[pl.ds(row * 4 + kk, 8, stride=64), :] for kk in range(4)]
-        ensemble = jnp.concatenate(tiles, axis=0)
-        mean = jnp.sum(ensemble, axis=0, keepdims=True) * (1.0 / K)
-        perturb = ensemble - mean
-        innovation = values[row : row + 1, :] - mean
-        weighted = perturb * weights[row : row + 1, :]
-        gram = lax.dot_general(
-            weighted,
-            jnp.concatenate([perturb] * 4, axis=0),
-            (((1,), (1,)), ((), ())),
-            precision=HIGHEST,
-            preferred_element_type=F32,
-        )
-        vector = jnp.sum(weighted * innovation, axis=1, keepdims=True)
-        terms = gram[0:8]
-        vecs = jnp.broadcast_to(vector[0:8], (8, LANES))
-        for kk in range(1, 4):
-            here = part == kk
-            terms = jnp.where(here, gram[kk * 8 : kk * 8 + 8], terms)
-            vecs = jnp.where(here, vector[kk * 8 : kk * 8 + 8], vecs)
-        out_ref[pl.ds(row, 8, stride=16), :] = jnp.where(slot, vecs, terms)
+    lane = iota((8, LANES), 1)
+    share = iota((8, LANES), 0)
+    for four in range(4):
+        perturbs, weighteds, vectors = [], [], []
+        for row in range(four * 4, four * 4 + 4):
+            tiles = [ens_ref[pl.ds(row * 4 + kk, 8, stride=64), :] for kk in range(4)]
+            ensemble = jnp.concatenate(tiles, axis=0)
+            mean = jnp.sum(ensemble, axis=0, keepdims=True) * (1.0 / K)
+            perturb = ensemble - mean
+            weighted = perturb * weights[row : row + 1, :]
+            innovation = values[row : row + 1, :] - mean
+            vectors.append(jnp.sum(weighted * innovation, axis=1, keepdims=True))
+            perturbs.append(perturb)
+            weighteds.append(weighted)
+        high, low = halves(jnp.concatenate(weighteds, axis=0))
+        right_high, right_low = halves(jnp.concatenate(perturbs, axis=0))
+        grams = dot_rows(
+            jnp.concatenate([high, low], axis=1), jnp.concatenate([right_high, right_high], axis=1)
+        ) + dot_rows(high, right_low)
+        terms = []
+        for j in range(4):
+            acc = None
+            for kk in range(4):
+                tile = grams[j * K + kk * 8 : j * K + kk * 8 + 8]
+                shift = (START[kk] - kk * 8 - j * K) % LANES
+                if shift:
+                    tile = pltpu.roll(tile, shift, 1)
+                slot = lane == START[kk] + low3(share + 1)
+                tile = jnp.where(slot, vectors[j][kk * 8 : kk * 8 + 8], tile)
+                acc = tile if acc is None else jnp.where(lane >= START[kk], tile, acc)
+            terms.append(acc)
+        for j in range(2):
+            even = terms[2 * j]
+            odd = pltpu.roll(terms[2 * j + 1], 64, 1)
+            main = jnp.where(lane < 64, even, odd)
+            rest = jnp.where(lane < 16, pltpu.roll(even, 64, 1), pltpu.roll(odd, 16, 1))
+            out_ref[pl.ds(four * 2 + j, 8, stride=16), :] = main
+            out_ref[pl.ds(8 + four * 2 + j, 8, stride=16), :] = rest
     for fetch in fetches:
         fetch.wait()
-    mix_ref[...] = mixing(slab_ref[0], weight_ref, block_ref, count_ref)
+    mixing(slab_ref[0], weight_ref, block_ref, count_ref, mix_ref)
 
 
 def window_kernel(in_ref, out_ref):
-    for jb in range(2):
-        rows = in_ref[pl.ds(jb, GRID, stride=2), :]
-        out_ref[pl.ds(2 + jb, GRID, stride=6), :] = rows
-        out_ref[pl.ds(jb, GRID, stride=6), :] = pltpu.roll(rows, 1, 0)
-        out_ref[pl.ds(4 + jb, GRID, stride=6), :] = pltpu.roll(rows, GRID - 1, 0)
+    main = jnp.concatenate([in_ref[m * 16 : m * 16 + 8] for m in range(8)], axis=0)
+    rest = jnp.concatenate([in_ref[m * 16 + 8 : m * 16 + 16] for m in range(8)], axis=0)
+    lane = iota((GRID, LANES), 1)
+    out_ref[pl.ds(0, GRID, stride=4), :] = pltpu.roll(main, 1, 0)
+    out_ref[pl.ds(1, GRID, stride=4), :] = main
+    out_ref[pl.ds(2, GRID, stride=4), :] = pltpu.roll(main, GRID - 1, 0)
+    before = pltpu.roll(rest, 1, 0)
+    after = pltpu.roll(pltpu.roll(rest, GRID - 1, 0), 64, 1)
+    here = pltpu.roll(rest, 32, 1)
+    out_ref[pl.ds(3, GRID, stride=4), :] = jnp.where(
+        lane < 32, before, jnp.where(lane < 64, here, after)
+    )
 
 
 def combine_kernel(in_ref, mix_ref, state_ref, out_ref, combo_ref):
+    lane = iota((GRID, LANES), 1)
+    rest = in_ref[pl.ds(3, GRID, stride=4), :]
+    rows = []
+    for d in range(3):
+        main = in_ref[pl.ds(d, GRID, stride=4), :]
+        for jb in range(2):
+            first = pltpu.roll(main, 64, 1) if jb else main
+            shift = (64 - d * 32 - jb * 16) % LANES
+            last = pltpu.roll(rest, shift, 1) if shift else rest
+            rows.append(jnp.where(lane < 64, first, last))
     combo_ref[...] = lax.dot_general(
         mix_ref[...],
-        in_ref[...],
+        jnp.concatenate(rows, axis=0),
         (((0,), (0,)), ((), ())),
         precision=HIGHEST,
         preferred_element_type=F32,
@@ -146,15 +190,6 @@
             out_ref[pl.ds(q * 2 + s0, 8, stride=24), :] = combo_ref[pl.ds(q * 16 + s0, 8, stride=2), :]
     for r in range(8):
         out_ref[pl.ds(16 + r, 8, stride=24), :] = state_ref[pl.ds(r, 8, stride=8), :]
-
-
-def halves(value):
-    high = value.astype(BF16)
-    return high, (value - high.astype(F32)).astype(BF16)
-
-
-def dot(left, right):
-    return jnp.dot(left, right, preferred_element_type=F32)
 
 
 def product(left, right, ones):
@@ -165,30 +200,35 @@
     return wide[:rows] + wide[rows:] + dot(high, right_low)
 
 
+def thirds(value):
+    high = value.astype(BF16)
+    rest = value - high.astype(F32)
+    middle = rest.astype(BF16)
+    return high, middle, (rest - middle.astype(F32)).astype(BF16)
+
+
 def segment_sum(value, ones):
-    high, rest = value.astype(BF16), value
-    rest = rest - high.astype(F32)
-    middle = rest.astype(BF16)
-    low = (rest - middle.astype(F32)).astype(BF16)
     rows = value.shape[0]
-    wide = dot(jnp.concatenate([high, middle, low], axis=0), ones)
+    wide = dot(jnp.concatenate(thirds(value), axis=0), ones)
     return wide[:rows] + wide[rows : 2 * rows] + wide[2 * rows :]
 
 
-def roll_segment(value, shift, column):
-    width = value.shape[1]
-    return jnp.where(
-        column >= shift, pltpu.roll(value, shift, 1), pltpu.roll(value, width - K + shift, 1)
-    )
+def mirrored(value, identity, ones):
+    total = 0.0
+    for third in thirds(value)[::-1]:
+        total = total + dot_rows(identity, jnp.concatenate([third] * Q, axis=0) * ones)
+    return total
 
 
 def transform_kernel(in_ref, out_ref):
     width = Q * K
     ones = (iota((width, width), 0) // K == iota((width, width), 1) // K).astype(F32).astype(BF16)
-    part = iota((8, LANES), 1) // K
+    lane = iota((8, LANES), 1)
     row = iota((K, width), 0)
     column = jnp.bitwise_and(iota((K, width), 1), K - 1)
-    slot = slot_mask(row, column)
+    diagonal = row // 8 == column // 8
+    slot = jnp.logical_and(diagonal, low3(column) == low3(row + 1))
+    keep = jnp.logical_or(row // 8 < column // 8, jnp.logical_and(diagonal, jnp.logical_not(slot)))
     identity = (row == column).astype(F32)
     point = iota((width, BV), 0) // K == iota((width, BV), 1) // (BV // Q)
     point = point.astype(F32).astype(BF16)
@@ -200,20 +240,25 @@
         for kk in range(4):
             sides = []
             for half in range(2):
-                acc = None
+                acc = jnp.zeros((8, LANES), F32)
                 for qq in range(4):
                     tile = tiles[half * 4 + qq]
-                    shift = (qq - kk) * K % LANES
+                    shift = (qq * K + kk * 8 - START[kk]) % LANES
                     if shift:
                         tile = pltpu.roll(tile, shift, 1)
-                    acc = tile if acc is None else jnp.where(part == qq, tile, acc)
+                    inside = jnp.logical_and(lane >= qq * K + kk * 8, lane < qq * K + K)
+                    acc = jnp.where(inside, tile, acc)
                 sides.append(acc)
             rows.append(jnp.concatenate(sides, axis=1))
         packed = jnp.concatenate(rows, axis=0)
-        mirror = roll_segment(jnp.concatenate(rows[1:] + rows[:1], axis=0), 8, column)
-        amats.append(jnp.where(slot, mirror, packed) + (K - 1.0) * identity)
+        flipped = mirrored(packed, identity.astype(BF16), ones)
+        amats.append(jnp.where(keep, packed, flipped) + (K - 1.0) * identity)
         drive = jnp.sum(jnp.where(slot, packed, 0.0), axis=0, keepdims=True)
-        drives.append(roll_segment(jnp.broadcast_to(drive, (8, width)), K - 8, column[:8])[:1])
+        drive = jnp.broadcast_to(drive, (8, width))
+        drive = jnp.where(
+            low3(column[:8]) == 7, pltpu.roll(drive, 7, 1), pltpu.roll(drive, width - 1, 1)
+        )
+        drives.append(drive[:1])
     squares = [
         jnp.broadcast_to(jnp.sum(amat * amat, axis=0, keepdims=True), (8, width)) for amat in amats
     ]
@@ -253,7 +298,7 @@
     gathered = swap(obs_ens.reshape(OB * 4, LANES), "member")
     terms, mix = call(
         terms_kernel,
-        (OB, 6 * GRID),
+        (OB, 3 * OB),
         slab,
         member,
         gathered,
@@ -271,8 +316,8 @@
         ],
     )
     shares = swap(terms, "member")
-    (windows,) = call(window_kernel, (6 * GRID,), shares)
-    arrived = swap(windows.reshape(3 * GRID, 2, LANES), "grid").reshape(6 * GRID, LANES)
+    (windows,) = call(window_kernel, (4 * GRID,), shares)
+    arrived = swap(windows.reshape(GRID, 4, LANES), "grid").reshape(4 * GRID, LANES)
     (combos,) = call(
         combine_kernel,
         (8 * 24,),

time: 80.3 us -> 78.2 us (0.974)
  blocking collectives: 56.6 us -> 54.7 us
    all_to_all x4, blocking collectives: 56.6 us -> 54.7 us  [swap(): return lax.all_to_all(array, axis, split_axis=0, concat_axis=0, tiled=True)]
where the time goes in v2:
time: 78.2 us; the launch traced here: 77.7 us
  blocking collectives  54.7 us (70%)
  starting transfers between devices  10.3 us (13%)
  waiting for transfers between devices  6.5 us (8%)
  Pallas kernels  5.56 us (7%)
    all_to_all x4, blocking collectives, swap(): return lax.all_to_all(array, axis, split_axis=0, concat_axis=0, tiled=True)  54.7 us
    all_to_all x1, starting transfers between devices, swap(): return lax.all_to_all(array, axis, split_axis=0, concat_axis=0, tiled=True)  10.3 us
    all_to_all x1, waiting for transfers between devices, swap(): return lax.all_to_all(array, axis, split_axis=0, concat_axis=0, tiled=True)  6.5 us
    pallas_call x4, Pallas kernels, call(): pl.pallas_call(kernel, out_shape=[jax.ShapeDtypeStruct((rows, LANES), F32...  5.56 us
  transfers between devices with their start and end apart: 1, of which 1 were waited for; matrix products, arithmetic and copies ran while one was open for 0% of the time, Pallas kernels for 0%

profile of v2, /device:TPU:1, one launch (start us, length us, event | category | flops | bytes accessed | tf_op | source)
XLA Modules:
  0.0 77.7 jit_solution(11777974704013117945)
XLA Ops:
  0.0 0.0 copy-start
  0.0 0.0 copy-start.1
  0.0 0.0 copy-start.3
  0.0 10.3 %all-to-all-start = ((f32[8,64,128]{2,1,0:T(8,128)}), f32[8,64,128]{2,1,0:T(8,128)S(1)}, u32[]{:S(2)}, u32[]{:S(2)}) async-start(f32[8,64,128]{2,1,0:T(8,128)} %bitcast.25), calls=%async_computation | async-start | bytes 524288 | tf_op jit(solution)/shard_map/all_to_all | solution.py:292
  10.3 6.5 %all-to-all-done = f32[8,64,128]{2,1,0:T(8,128)S(1)} async-done(((f32[8,64,128]{2,1,0:T(8,128)}), f32[8,64,128]{2,1,0:T(8,128)S(1)}, u32[]{:S(2)}, u32[]{:S(2)}) %all-to-all-start) | async-done | bytes 262176 | tf_op jit(solution)/shard_map/all_to_all | solution.py:292
  16.8 0.0 copy-done
  16.8 0.0 copy-done.1
  16.8 0.0 copy-done.3
  16.8 1.4 %terms_kernel.1 = (f32[128,128]{1,0:T(8,128)S(1)}, f32[384,128]{1,0:T(8,128)S(1)}) custom-call(s32[1]{0:T(128)} %bitcast.slab_ref, s32[1]{0:T(128)} %bitcast.1.member_ref, f32[512,128]{1,0:T(8,128)S(1)} %bitcast.15, f32[128,128]{1,0:T(8,128)S(1)} %copy-done, f32[128,128]{1,0:T(8,128)S(1)} %copy-done.1, f32[8,8,16]{2,1,0:T(8,128)S(1)} %bitcast.24, ...), custom_call_target="tpu_custom_call" | custom-call | tf_op jit(solution)/shard_map/terms_kernel/pallas_call | solution.py:53
  18.2 8.3 %all_to_all.43 = f32[8,16,128]{2,1,0:T(8,128)S(1)} all-to-all(f32[8,16,128]{2,1,0:T(8,128)S(1)} %bitcast.22), channel_id=1, replica_groups=mesh['grid'=64,'member'=8] {'member'}, dimensions={0} | all-to-all | bytes 131072 | tf_op jit(solution)/shard_map/all_to_all | solution.py:292
  26.4 0.1 window_kernel.1
  26.5 0.0 copy-start.2
  26.6 28.1 %all_to_all.44 = f32[64,4,128]{2,1,0:T(4,128)S(1)} all-to-all(f32[64,4,128]{2,1,0:T(4,128)S(1)} %bitcast.17), channel_id=1, replica_groups=mesh['grid'=64,'member'=8] {'grid'}, dimensions={0} | all-to-all | bytes 262144 | tf_op jit(solution)/shard_map/all_to_all | solution.py:292
  54.6 0.0 copy-done.2
  54.6 0.5 combine_kernel.1
  55.1 10.5 %all_to_all.45 = f32[8,24,128]{2,1,0:T(8,128)S(1)} all-to-all(f32[8,24,128]{2,1,0:T(8,128)S(1)} %bitcast.18), channel_id=1, replica_groups=mesh['grid'=64,'member'=8] {'member'}, dimensions={0} | all-to-all | bytes 196608 | tf_op jit(solution)/shard_map/all_to_all | solution.py:292
  65.6 3.6 %transform_kernel.1 = f32[64,128]{1,0:T(8,128)S(1)} custom-call(f32[192,128]{1,0:T(8,128)S(1)} %bitcast.19), custom_call_target="tpu_custom_call" | custom-call | tf_op jit(solution)/shard_map/transform_kernel/pallas_call | solution.py:53
  69.2 7.9 %all_to_all.46 = f32[16,4,128]{2,1,0:T(4,128)S(1)} all-to-all(f32[16,4,128]{2,1,0:T(4,128)S(1)} %bitcast.21), channel_id=1, replica_groups=mesh['grid'=64,'member'=8] {'member'}, dimensions={0} | all-to-all | bytes 65536 | tf_op jit(solution)/shard_map/all_to_all | solution.py:292
  77.1 0.6 copy.9
Async XLA Ops:
  0.0 16.8 %copy-start = (f32[128,128]{1,0:T(8,128)S(1)}, f32[128,128]{1,0:T(8,128)}, u32[]{:S(2)}) copy-start(f32[128,128]{1,0:T(8,128)} %value_ref.1) | copy-start | bytes 196612
  0.0 16.8 %copy-start.1 = (f32[128,128]{1,0:T(8,128)S(1)}, f32[128,128]{1,0:T(8,128)}, u32[]{:S(2)}) copy-start(f32[128,128]{1,0:T(8,128)} %rinv_ref.1) | copy-start | bytes 196612
  0.0 16.8 %copy-start.3 = (f32[16,8,8]{0,2,1:T(8,128)S(1)}, f32[16,8,8]{0,2,1:T(8,128)}, u32[]{:S(2)}) copy-start(f32[16,8,8]{0,2,1:T(8,128)} %param.11) | copy-start | bytes 12292
  0.0 16.8 %all-to-all-start = ((f32[8,64,128]{2,1,0:T(8,128)}), f32[8,64,128]{2,1,0:T(8,128)S(1)}, u32[]{:S(2)}, u32[]{:S(2)}) async-start(f32[8,64,128]{2,1,0:T(8,128)} %bitcast.25), calls=%async_computation | async-start | bytes 524288 | tf_op jit(solution)/shard_map/all_to_all | solution.py:292
  26.5 28.1 %copy-start.2 = (f32[16,4,128]{2,1,0:T(4,128)S(1)}, f32[16,4,128]{2,1,0:T(4,128)}, u32[]{:S(2)}) copy-start(f32[16,4,128]{2,1,0:T(4,128)} %param.7) | copy-start | bytes 98308

commit v3 on v2

--- a/solution.py
+++ b/solution.py
@@ -47,16 +47,18 @@
     return lax.dot_general(left, right, (((1,), (1,)), ((), ())), preferred_element_type=F32)
 
 
-def call(kernel, out_rows, *args, scalars=0, unplaced=0, scratch=()):
+def call(kernel, outs, *args, scalars=0, unplaced=0, scratch=()):
     vmem = pl.BlockSpec(memory_space=pltpu.VMEM)
-    placed = [vmem] * (len(args) - scalars - unplaced)
     return pl.pallas_call(
         kernel,
-        out_shape=[jax.ShapeDtypeStruct((rows, LANES), F32) for rows in out_rows],
+        out_shape=[
+            out if isinstance(out, jax.ShapeDtypeStruct) else jax.ShapeDtypeStruct((out, LANES), F32)
+            for out in outs
+        ],
         in_specs=[pl.BlockSpec(memory_space=pltpu.SMEM)] * scalars
-        + placed
-        + [pl.BlockSpec(memory_space=pltpu.HBM)] * unplaced,
-        out_specs=[vmem] * len(out_rows),
+        + [vmem] * (len(args) - scalars - unplaced)
+        + [pl.BlockSpec(memory_space=pl.ANY)] * unplaced,
+        out_specs=[vmem] * len(outs),
         scratch_shapes=scratch,
         compiler_params=pltpu.CompilerParams(vmem_limit_bytes=VMEM_BYTES),
         interpret=INTERPRET,
@@ -64,15 +66,11 @@
     )(*args)
 
 
-def hold(array):
-    return array if INTERPRET else pltpu.with_memory_space_constraint(array, pltpu.HBM)
-
-
-def mixing(slab, weight_ref, block_ref, count_ref, mix_ref):
+def mix_kernel(slab_ref, weight_ref, block_ref, count_ref, out_ref, mix_ref):
     picked = jnp.concatenate([block_ref[...]] * Q, axis=1)
     weight = jnp.concatenate([weight_ref[q] for q in range(Q)], axis=1)
     count = jnp.concatenate([count_ref[...]] * Q, axis=1)
-    target = slab * OB + picked - OB
+    target = slab_ref[0] * OB + picked - OB
     used = jnp.logical_and(target >= 0, target < GRID * OB)
     used = jnp.logical_and(used, iota((P_SIZE, LANES), 0) < count)
     weight = jnp.where(used, weight, 0.0)
@@ -83,29 +81,10 @@
         for p in range(P_SIZE):
             mix = mix + jnp.where(block + first == picked[p : p + 1], weight[p : p + 1], 0.0)
         mix_ref[first : first + step] = mix
-
-
-def terms_kernel(
-    slab_ref,
-    member_ref,
-    ens_ref,
-    value_ref,
-    rinv_ref,
-    weight_ref,
-    block_hbm,
-    count_hbm,
-    out_ref,
-    mix_ref,
-    block_ref,
-    count_ref,
-    sems,
-):
-    fetches = [
-        pltpu.make_async_copy(block_hbm, block_ref, sems.at[0]),
-        pltpu.make_async_copy(count_hbm, count_ref, sems.at[1]),
-    ]
-    for fetch in fetches:
-        fetch.start()
+    out_ref[...] = jnp.concatenate(halves(jnp.transpose(mix_ref[...])), axis=1)
+
+
+def terms_kernel(member_ref, ens_ref, value_ref, rinv_ref, _, out_ref):
     start = pl.multiple_of(member_ref[0] * 16, 16)
     values = value_ref[pl.ds(start, 16), :]
     weights = rinv_ref[pl.ds(start, 16), :]
@@ -147,9 +126,6 @@
             rest = jnp.where(lane < 16, pltpu.roll(even, 64, 1), pltpu.roll(odd, 16, 1))
             out_ref[pl.ds(four * 2 + j, 8, stride=16), :] = main
             out_ref[pl.ds(8 + four * 2 + j, 8, stride=16), :] = rest
-    for fetch in fetches:
-        fetch.wait()
-    mixing(slab_ref[0], weight_ref, block_ref, count_ref, mix_ref)
 
 
 def window_kernel(in_ref, out_ref):
@@ -178,13 +154,9 @@
             shift = (64 - d * 32 - jb * 16) % LANES
             last = pltpu.roll(rest, shift, 1) if shift else rest
             rows.append(jnp.where(lane < 64, first, last))
-    combo_ref[...] = lax.dot_general(
-        mix_ref[...],
-        jnp.concatenate(rows, axis=0),
-        (((0,), (0,)), ((), ())),
-        precision=HIGHEST,
-        preferred_element_type=F32,
-    )
+    high, low = halves(jnp.concatenate(rows, axis=0))
+    mix = mix_ref[...]
+    combo_ref[...] = dot(mix, jnp.concatenate([high, high], axis=0)) + dot(mix[:, : 3 * OB], low)
     for q in range(Q):
         for s0 in range(2):
             out_ref[pl.ds(q * 2 + s0, 8, stride=24), :] = combo_ref[pl.ds(q * 16 + s0, 8, stride=2), :]
@@ -192,12 +164,20 @@
         out_ref[pl.ds(16 + r, 8, stride=24), :] = state_ref[pl.ds(r, 8, stride=8), :]
 
 
-def product(left, right, ones):
+def spread(value, mask):
+    blocks = mask.shape[0] // value.shape[0]
+    return jnp.concatenate(
+        [jnp.concatenate([half] * blocks, axis=0) * mask for half in halves(value)], axis=1
+    )
+
+
+def product(left, right):
+    columns = right.shape[1] // 2
     high, low = halves(left)
-    right_high, right_low = (jnp.concatenate([half] * Q, axis=0) * ones for half in halves(right))
-    rows = left.shape[0]
-    wide = dot(jnp.concatenate([high, low], axis=0), right_high)
-    return wide[:rows] + wide[rows:] + dot(high, right_low)
+    return dot(
+        jnp.concatenate([high, low], axis=1),
+        jnp.concatenate([right[:, :columns]] * 2, axis=0),
+    ) + dot(high, right[:, columns:])
 
 
 def thirds(value):
@@ -214,76 +194,78 @@
 
 
 def mirrored(value, identity, ones):
-    total = 0.0
-    for third in thirds(value)[::-1]:
-        total = total + dot_rows(identity, jnp.concatenate([third] * Q, axis=0) * ones)
-    return total
+    high, middle, low = [jnp.concatenate([third] * 4, axis=0) * ones for third in thirds(value)]
+    return dot_rows(
+        jnp.concatenate([identity] * 2, axis=1), jnp.concatenate([high, middle], axis=1)
+    ) + dot_rows(identity, low)
 
 
 def transform_kernel(in_ref, out_ref):
-    width = Q * K
-    ones = (iota((width, width), 0) // K == iota((width, width), 1) // K).astype(F32).astype(BF16)
+    def same(shape, rows, lanes):
+        return (iota(shape, 0) // rows == iota(shape, 1) // lanes).astype(F32).astype(BF16)
+
+    ones = same((LANES, LANES), K, K)
+    point = same((Q * K, BV), K, BV // Q)
     lane = iota((8, LANES), 1)
-    row = iota((K, width), 0)
-    column = jnp.bitwise_and(iota((K, width), 1), K - 1)
+    row = iota((K, LANES), 0)
+    column = jnp.bitwise_and(iota((K, LANES), 1), K - 1)
     diagonal = row // 8 == column // 8
     slot = jnp.logical_and(diagonal, low3(column) == low3(row + 1))
     keep = jnp.logical_or(row // 8 < column // 8, jnp.logical_and(diagonal, jnp.logical_not(slot)))
     identity = (row == column).astype(F32)
-    point = iota((width, BV), 0) // K == iota((width, BV), 1) // (BV // Q)
-    point = point.astype(F32).astype(BF16)
-    pair = range(2)
-    amats, drives = [], []
-    for s0 in pair:
-        tiles = [in_ref[pl.ds(q * 2 + s0, 8, stride=24), :] for q in range(Q)]
+    mirror = jnp.logical_and(diagonal, low3(row) == low3(column + 1))
+    times = jnp.where(diagonal, jnp.where(slot, 0.0, jnp.where(mirror, 2.0, 1.0)), 2.0)
+    groups = range(4)
+    amats, drives, squares = [], [], []
+    for g in groups:
+        tiles = [in_ref[pl.ds((g % 2 * 4 + qq) * 2 + g // 2, 8, stride=24), :] for qq in range(4)]
         rows = []
         for kk in range(4):
-            sides = []
-            for half in range(2):
-                acc = jnp.zeros((8, LANES), F32)
-                for qq in range(4):
-                    tile = tiles[half * 4 + qq]
-                    shift = (qq * K + kk * 8 - START[kk]) % LANES
-                    if shift:
-                        tile = pltpu.roll(tile, shift, 1)
-                    inside = jnp.logical_and(lane >= qq * K + kk * 8, lane < qq * K + K)
-                    acc = jnp.where(inside, tile, acc)
-                sides.append(acc)
-            rows.append(jnp.concatenate(sides, axis=1))
+            acc = jnp.zeros((8, LANES), F32)
+            for qq in range(4):
+                tile = tiles[qq]
+                shift = (qq * K + kk * 8 - START[kk]) % LANES
+                if shift:
+                    tile = pltpu.roll(tile, shift, 1)
+                inside = jnp.logical_and(lane >= qq * K + kk * 8, lane < qq * K + K)
+                acc = jnp.where(inside, tile, acc)
+            rows.append(acc)
         packed = jnp.concatenate(rows, axis=0)
         flipped = mirrored(packed, identity.astype(BF16), ones)
         amats.append(jnp.where(keep, packed, flipped) + (K - 1.0) * identity)
+        square = packed + (K - 1.0) * identity
+        square = jnp.sum(square * square * times, axis=0, keepdims=True)
+        squares.append(jnp.broadcast_to(square, (8, LANES)))
         drive = jnp.sum(jnp.where(slot, packed, 0.0), axis=0, keepdims=True)
-        drive = jnp.broadcast_to(drive, (8, width))
-        drive = jnp.where(
-            low3(column[:8]) == 7, pltpu.roll(drive, 7, 1), pltpu.roll(drive, width - 1, 1)
-        )
+        drive = jnp.broadcast_to(drive, (8, LANES))
+        drive = jnp.where(low3(lane) == 7, pltpu.roll(drive, 7, 1), pltpu.roll(drive, LANES - 1, 1))
         drives.append(drive[:1])
-    squares = [
-        jnp.broadcast_to(jnp.sum(amat * amat, axis=0, keepdims=True), (8, width)) for amat in amats
-    ]
     sums = segment_sum(jnp.concatenate(squares, axis=0), ones)
-    frobenius = [jnp.sqrt(sums[8 * s0 : 8 * s0 + 1]) for s0 in pair]
-    root = [amats[s0] / frobenius[s0] for s0 in pair]
-    inverse = [1.5 * identity - 0.5 * root[s0] for s0 in pair]
-    root = [product(root[s0], inverse[s0], ones) for s0 in pair]
-    for _ in range(1, NS - 1):
-        middle = [1.5 * identity - 0.5 * product(inverse[s0], root[s0], ones) for s0 in pair]
-        both = [
-            product(jnp.concatenate([root[s0], inverse[s0]], axis=0), middle[s0], ones) for s0 in pair
-        ]
-        root = [both[s0][:K] for s0 in pair]
-        inverse = [both[s0][K:] for s0 in pair]
-    middle = [1.5 * identity - 0.5 * product(inverse[s0], root[s0], ones) for s0 in pair]
-    inverse = [product(inverse[s0], middle[s0], ones) for s0 in pair]
-    first = [segment_sum(inverse[s0] * drives[s0], ones) for s0 in pair]
-    for s0 in pair:
-        wmean = jnp.sum(inverse[s0] * first[s0], axis=0, keepdims=True) / frobenius[s0]
-        trans = inverse[s0] * (jnp.sqrt(K - 1.0) / jnp.sqrt(frobenius[s0])) + wmean
+    frobenius = [jnp.sqrt(sums[8 * g : 8 * g + 1]) for g in groups]
+    root = [amats[g] / frobenius[g] for g in groups]
+    inverse = [1.5 * identity - 0.5 * root[g] for g in groups]
+    for step in range(NS - 1):
+        blocks = [spread(root[g], ones) for g in groups]
+        if step == 0:
+            square = [product(root[g], blocks[g]) for g in groups]
+        else:
+            square = [product(root[g], blocks[g]) for g in groups]
+            inverse = [1.5 * inverse[g] - 0.5 * product(inverse[g], blocks[g]) for g in groups]
+        middle = [2.25 * identity - 1.5 * root[g] + 0.25 * square[g] for g in groups]
+        root = [product(middle[g], blocks[g]) for g in groups]
+    blocks = [spread(root[g], ones) for g in groups]
+    inverse = [1.5 * inverse[g] - 0.5 * product(inverse[g], blocks[g]) for g in groups]
+    for s0 in range(2):
+        both = slice(2 * s0, 2 * s0 + 2)
+        wide = jnp.concatenate(inverse[both], axis=1)
         state = jnp.concatenate(
             [in_ref[pl.ds(16 + s0 * 4 + kk, 8, stride=24), :] for kk in range(4)], axis=0
         )
-        update = product(trans, state, point)
+        moved = product(wide, spread(state, point))
+        first = segment_sum(wide * jnp.concatenate(drives[both], axis=1), point)
+        norm = jnp.sqrt(segment_sum(jnp.concatenate(squares[both], axis=1), point)[:1])
+        shift = jnp.sum(first * moved, axis=0, keepdims=True) / norm
+        update = moved * (jnp.sqrt(K - 1.0) / jnp.sqrt(norm)) + shift
         for kk in range(4):
             out_ref[pl.ds(s0 * 4 + kk, 8, stride=8), :] = update[kk * 8 : kk * 8 + 8]
 
@@ -296,24 +278,18 @@
     slab = lax.axis_index("grid").astype(jnp.int32).reshape(1)
     member = lax.axis_index("member").astype(jnp.int32).reshape(1)
     gathered = swap(obs_ens.reshape(OB * 4, LANES), "member")
-    terms, mix = call(
-        terms_kernel,
-        (OB, 3 * OB),
+    (mix,) = call(
+        mix_kernel,
+        (jax.ShapeDtypeStruct((LANES, 6 * OB), BF16),),
         slab,
-        member,
-        gathered,
-        obs_value,
-        obs_rinv,
         jnp.transpose(loc_weight, (1, 2, 0)),
-        hold(jnp.transpose(pair_block, (1, 0))),
-        hold(pair_count.reshape(1, SB)),
-        scalars=2,
-        unplaced=2,
-        scratch=[
-            pltpu.VMEM((P_SIZE, SB), jnp.int32),
-            pltpu.VMEM((1, SB), jnp.int32),
-            pltpu.SemaphoreType.DMA((2,)),
-        ],
+        jnp.transpose(pair_block, (1, 0)),
+        pair_count.reshape(1, SB),
+        scalars=1,
+        scratch=[pltpu.VMEM((3 * OB, LANES), F32)],
+    )
+    (terms,) = call(
+        terms_kernel, (OB,), member, gathered, obs_value, obs_rinv, mix, scalars=1, unplaced=1
     )
     shares = swap(terms, "member")
     (windows,) = call(window_kernel, (4 * GRID,), shares)

time: 78.2 us -> 76 us (0.972)
  Pallas kernels: 5.56 us -> 3.77 us
  waiting for transfers between devices: 6.5 us -> 5.47 us
    pallas_call x4 -> x5, Pallas kernels: 5.56 us -> 3.77 us  [call(): pl.pallas_call(kernel, out_shape=[out if isinstance(out, jax.ShapeDtypeSt...]
    all_to_all x1, waiting for transfers between devices: 6.5 us -> 5.47 us  [swap(): return lax.all_to_all(array, axis, split_axis=0, concat_axis=0, tiled=True)]
where the time goes in v3:
time: 76 us; the launch traced here: 75.6 us
  blocking collectives  54.7 us (72%)
  starting transfers between devices  10.3 us (14%)
  waiting for transfers between devices  5.47 us (7%)
  Pallas kernels  3.77 us (5%)
  local copies, waits for them, and re-layouts  1.31 us (2%)
    all_to_all x4, blocking collectives, swap(): return lax.all_to_all(array, axis, split_axis=0, concat_axis=0, tiled=True)  54.7 us
    all_to_all x1, starting transfers between devices, swap(): return lax.all_to_all(array, axis, split_axis=0, concat_axis=0, tiled=True)  10.3 us
    all_to_all x1, waiting for transfers between devices, swap(): return lax.all_to_all(array, axis, split_axis=0, concat_axis=0, tiled=True)  5.47 us
    pallas_call x5, Pallas kernels, call(): pl.pallas_call(kernel, out_shape=[out if isinstance(out, jax.ShapeDtypeSt...  3.77 us
  transfers between devices with their start and end apart: 1, of which 1 were waited for; matrix products, arithmetic and copies ran while one was open for 0% of the time, Pallas kernels for 0%

profile of v3, /device:TPU:1, one launch (start us, length us, event | category | flops | bytes accessed | tf_op | source)
XLA Modules:
  0.0 75.6 jit_solution(14289109188693181946)
XLA Ops:
  0.0 0.0 copy-start.3
  0.0 10.3 %all-to-all-start = ((f32[8,64,128]{2,1,0:T(8,128)}), f32[8,64,128]{2,1,0:T(8,128)S(1)}, u32[]{:S(2)}, u32[]{:S(2)}) async-start(f32[8,64,128]{2,1,0:T(8,128)} %bitcast.27), calls=%async_computation | async-start | bytes 524288 | tf_op jit(solution)/shard_map/all_to_all | solution.py:274
  10.3 0.0 copy-start.4
  10.3 0.0 copy-start.5
  10.3 0.0 copy-done.3
  10.3 0.7 copy-done.4
  11.0 0.0 copy-done.5
  11.0 0.0 copy-start
  11.0 0.0 copy-start.1
  11.0 0.3 mix_kernel.1._.mix_ref
  11.3 5.5 %all-to-all-done = f32[8,64,128]{2,1,0:T(8,128)S(1)} async-done(((f32[8,64,128]{2,1,0:T(8,128)}), f32[8,64,128]{2,1,0:T(8,128)S(1)}, u32[]{:S(2)}, u32[]{:S(2)}) %all-to-all-start) | async-done | bytes 262176 | tf_op jit(solution)/shard_map/all_to_all | solution.py:274
  16.8 0.0 copy-done
  16.8 0.0 copy-done.1
  16.8 0.6 terms_kernel.1
  17.4 8.3 %all_to_all.43 = f32[8,16,128]{2,1,0:T(8,128)S(1)} all-to-all(f32[8,16,128]{2,1,0:T(8,128)S(1)} %bitcast.20), channel_id=1, replica_groups=mesh['grid'=64,'member'=8] {'member'}, dimensions={0} | all-to-all | bytes 131072 | tf_op jit(solution)/shard_map/all_to_all | solution.py:274
  25.6 0.1 window_kernel.1
  25.7 0.0 copy-start.2
  25.7 28.1 %all_to_all.44 = f32[64,4,128]{2,1,0:T(4,128)S(1)} all-to-all(f32[64,4,128]{2,1,0:T(4,128)S(1)} %bitcast.17), channel_id=1, replica_groups=mesh['grid'=64,'member'=8] {'grid'}, dimensions={0} | all-to-all | bytes 262144 | tf_op jit(solution)/shard_map/all_to_all | solution.py:274
  53.8 0.0 copy-done.2
  53.8 0.4 combine_kernel.1
  54.1 10.5 %all_to_all.45 = f32[8,24,128]{2,1,0:T(8,128)S(1)} all-to-all(f32[8,24,128]{2,1,0:T(8,128)S(1)} %bitcast.18), channel_id=1, replica_groups=mesh['grid'=64,'member'=8] {'member'}, dimensions={0} | all-to-all | bytes 196608 | tf_op jit(solution)/shard_map/all_to_all | solution.py:274
  64.6 2.4 %transform_kernel.1 = f32[64,128]{1,0:T(8,128)S(1)} custom-call(f32[192,128]{1,0:T(8,128)S(1)} %bitcast.19), custom_call_target="tpu_custom_call" | custom-call | tf_op jit(solution)/shard_map/transform_kernel/pallas_call | solution.py:52
  67.0 7.9 %all_to_all.46 = f32[16,4,128]{2,1,0:T(4,128)S(1)} all-to-all(f32[16,4,128]{2,1,0:T(4,128)S(1)} %bitcast.22), channel_id=1, replica_groups=mesh['grid'=64,'member'=8] {'member'}, dimensions={0} | all-to-all | bytes 65536 | tf_op jit(solution)/shard_map/all_to_all | solution.py:274
  74.9 0.6 copy.9
Async XLA Ops:
  0.0 10.3 %copy-start.3 = (f32[16,8,8]{0,2,1:T(8,128)S(1)}, f32[16,8,8]{0,2,1:T(8,128)}, u32[]{:S(2)}) copy-start(f32[16,8,8]{0,2,1:T(8,128)} %param.11) | copy-start | bytes 12292
  0.0 16.8 %all-to-all-start = ((f32[8,64,128]{2,1,0:T(8,128)}), f32[8,64,128]{2,1,0:T(8,128)S(1)}, u32[]{:S(2)}, u32[]{:S(2)}) async-start(f32[8,64,128]{2,1,0:T(8,128)} %bitcast.27), calls=%async_computation | async-start | bytes 524288 | tf_op jit(solution)/shard_map/all_to_all | solution.py:274
  10.3 0.7 copy-start.4
  10.3 0.7 copy-start.5
  11.0 5.8 %copy-start = (f32[128,128]{1,0:T(8,128)S(1)}, f32[128,128]{1,0:T(8,128)}, u32[]{:S(2)}) copy-start(f32[128,128]{1,0:T(8,128)} %value_ref.1) | copy-start | bytes 196612
  11.0 5.8 %copy-start.1 = (f32[128,128]{1,0:T(8,128)S(1)}, f32[128,128]{1,0:T(8,128)}, u32[]{:S(2)}) copy-start(f32[128,128]{1,0:T(8,128)} %rinv_ref.1) | copy-start | bytes 196612
  25.7 28.1 %copy-start.2 = (f32[16,4,128]{2,1,0:T(4,128)S(1)}, f32[16,4,128]{2,1,0:T(4,128)}, u32[]{:S(2)}) copy-start(f32[16,4,128]{2,1,0:T(4,128)} %param.7) | copy-start | bytes 98308

commit v4 on v3

--- a/solution.py
+++ b/solution.py
@@ -34,9 +34,11 @@
     return jnp.bitwise_and(value, 7)
 
 
-def halves(value):
+def thirds(value):
     high = value.astype(BF16)
-    return high, (value - high.astype(F32)).astype(BF16)
+    rest = value - high.astype(F32)
+    middle = rest.astype(BF16)
+    return high, middle, (rest - middle.astype(F32)).astype(BF16)
 
 
 def dot(left, right):
@@ -45,6 +47,17 @@
 
 def dot_rows(left, right):
     return lax.dot_general(left, right, (((1,), (1,)), ((), ())), preferred_element_type=F32)
+
+
+def product(left, right, form, axis):
+    high, middle, low = left
+    first, second, third = right
+    both = jnp.concatenate([high, middle], axis=1)
+    return (
+        form(both, jnp.concatenate([first] * 2, axis=axis))
+        + form(both, jnp.concatenate([second] * 2, axis=axis))
+        + form(jnp.concatenate([low, high], axis=1), jnp.concatenate([first, third], axis=axis))
+    )
 
 
 def call(kernel, outs, *args, scalars=0, unplaced=0, scratch=()):
@@ -81,7 +94,7 @@
         for p in range(P_SIZE):
             mix = mix + jnp.where(block + first == picked[p : p + 1], weight[p : p + 1], 0.0)
         mix_ref[first : first + step] = mix
-    out_ref[...] = jnp.concatenate(halves(jnp.transpose(mix_ref[...])), axis=1)
+    out_ref[...] = jnp.concatenate(thirds(jnp.transpose(mix_ref[...])), axis=1)
 
 
 def terms_kernel(member_ref, ens_ref, value_ref, rinv_ref, _, out_ref):
@@ -102,11 +115,12 @@
             vectors.append(jnp.sum(weighted * innovation, axis=1, keepdims=True))
             perturbs.append(perturb)
             weighteds.append(weighted)
-        high, low = halves(jnp.concatenate(weighteds, axis=0))
-        right_high, right_low = halves(jnp.concatenate(perturbs, axis=0))
-        grams = dot_rows(
-            jnp.concatenate([high, low], axis=1), jnp.concatenate([right_high, right_high], axis=1)
-        ) + dot_rows(high, right_low)
+        grams = product(
+            thirds(jnp.concatenate(weighteds, axis=0)),
+            thirds(jnp.concatenate(perturbs, axis=0)),
+            dot_rows,
+            1,
+        )
         terms = []
         for j in range(4):
             acc = None
@@ -154,9 +168,13 @@
             shift = (64 - d * 32 - jb * 16) % LANES
             last = pltpu.roll(rest, shift, 1) if shift else rest
             rows.append(jnp.where(lane < 64, first, last))
-    high, low = halves(jnp.concatenate(rows, axis=0))
+    high, middle, low = thirds(jnp.concatenate(rows, axis=0))
     mix = mix_ref[...]
-    combo_ref[...] = dot(mix, jnp.concatenate([high, high], axis=0)) + dot(mix[:, : 3 * OB], low)
+    combo_ref[...] = (
+        dot(mix, jnp.concatenate([high] * 3, axis=0))
+        + dot(mix[:, : 6 * OB], jnp.concatenate([middle] * 2, axis=0))
+        + dot(mix[:, : 3 * OB], low)
+    )
     for q in range(Q):
         for s0 in range(2):
             out_ref[pl.ds(q * 2 + s0, 8, stride=24), :] = combo_ref[pl.ds(q * 16 + s0, 8, stride=2), :]
@@ -166,25 +184,7 @@
 
 def spread(value, mask):
     blocks = mask.shape[0] // value.shape[0]
-    return jnp.concatenate(
-        [jnp.concatenate([half] * blocks, axis=0) * mask for half in halves(value)], axis=1
-    )
-
-
-def product(left, right):
-    columns = right.shape[1] // 2
-    high, low = halves(left)
-    return dot(
-        jnp.concatenate([high, low], axis=1),
-        jnp.concatenate([right[:, :columns]] * 2, axis=0),
-    ) + dot(high, right[:, columns:])
-
-
-def thirds(value):
-    high = value.astype(BF16)
-    rest = value - high.astype(F32)
-    middle = rest.astype(BF16)
-    return high, middle, (rest - middle.astype(F32)).astype(BF16)
+    return [jnp.concatenate([third] * blocks, axis=0) * mask for third in thirds(value)]
 
 
 def segment_sum(value, ones):
@@ -247,21 +247,21 @@
     for step in range(NS - 1):
         blocks = [spread(root[g], ones) for g in groups]
         if step == 0:
-            square = [product(root[g], blocks[g]) for g in groups]
+            square = [product(thirds(root[g]), blocks[g], dot, 0) for g in groups]
         else:
-            square = [product(root[g], blocks[g]) for g in groups]
-            inverse = [1.5 * inverse[g] - 0.5 * product(inverse[g], blocks[g]) for g in groups]
+            square = [product(thirds(root[g]), blocks[g], dot, 0) for g in groups]
+            inverse = [1.5 * inverse[g] - 0.5 * product(thirds(inverse[g]), blocks[g], dot, 0) for g in groups]
         middle = [2.25 * identity - 1.5 * root[g] + 0.25 * square[g] for g in groups]
-        root = [product(middle[g], blocks[g]) for g in groups]
+        root = [product(thirds(middle[g]), blocks[g], dot, 0) for g in groups]
     blocks = [spread(root[g], ones) for g in groups]
-    inverse = [1.5 * inverse[g] - 0.5 * product(inverse[g], blocks[g]) for g in groups]
+    inverse = [1.5 * inverse[g] - 0.5 * product(thirds(inverse[g]), blocks[g], dot, 0) for g in groups]
     for s0 in range(2):
         both = slice(2 * s0, 2 * s0 + 2)
         wide = jnp.concatenate(inverse[both], axis=1)
         state = jnp.concatenate(
             [in_ref[pl.ds(16 + s0 * 4 + kk, 8, stride=24), :] for kk in range(4)], axis=0
         )
-        moved = product(wide, spread(state, point))
+        moved = product(thirds(wide), spread(state, point), dot, 0)
         first = segment_sum(wide * jnp.concatenate(drives[both], axis=1), point)
         norm = jnp.sqrt(segment_sum(jnp.concatenate(squares[both], axis=1), point)[:1])
         shift = jnp.sum(first * moved, axis=0, keepdims=True) / norm
@@ -280,7 +280,7 @@
     gathered = swap(obs_ens.reshape(OB * 4, LANES), "member")
     (mix,) = call(
         mix_kernel,
-        (jax.ShapeDtypeStruct((LANES, 6 * OB), BF16),),
+        (jax.ShapeDtypeStruct((LANES, 9 * OB), BF16),),
         slab,
         jnp.transpose(loc_weight, (1, 2, 0)),
         jnp.transpose(pair_block, (1, 0)),

time: 76 us -> 76.9 us (1.012)
  Pallas kernels: 3.77 us -> 4.6 us
    pallas_call x5, Pallas kernels: 3.77 us -> 4.6 us  [call(): pl.pallas_call(kernel, out_shape=[out if isinstance(out, jax.ShapeDtypeSt...]
where the time goes in v4:
time: 76.9 us; the launch traced here: 76.4 us
  blocking collectives  54.7 us (71%)
  starting transfers between devices  10.3 us (13%)
  waiting for transfers between devices  5.47 us (7%)
  Pallas kernels  4.6 us (6%)
  local copies, waits for them, and re-layouts  1.31 us (2%)
    all_to_all x4, blocking collectives, swap(): return lax.all_to_all(array, axis, split_axis=0, concat_axis=0, tiled=True)  54.7 us
    all_to_all x1, starting transfers between devices, swap(): return lax.all_to_all(array, axis, split_axis=0, concat_axis=0, tiled=True)  10.3 us
    all_to_all x1, waiting for transfers between devices, swap(): return lax.all_to_all(array, axis, split_axis=0, concat_axis=0, tiled=True)  5.47 us
    pallas_call x5, Pallas kernels, call(): pl.pallas_call(kernel, out_shape=[out if isinstance(out, jax.ShapeDtypeSt...  4.6 us
  transfers between devices with their start and end apart: 1, of which 1 were waited for; matrix products, arithmetic and copies ran while one was open for 0% of the time, Pallas kernels for 0%

profile of v4, /device:TPU:1, one launch (start us, length us, event | category | flops | bytes accessed | tf_op | source)
XLA Modules:
  0.0 76.4 jit_solution(8627369091195157710)
XLA Ops:
  0.0 0.0 copy-start.3
  0.0 10.3 %all-to-all-start = ((f32[8,64,128]{2,1,0:T(8,128)}), f32[8,64,128]{2,1,0:T(8,128)S(1)}, u32[]{:S(2)}, u32[]{:S(2)}) async-start(f32[8,64,128]{2,1,0:T(8,128)} %bitcast.27), calls=%async_computation | async-start | bytes 524288 | tf_op jit(solution)/shard_map/all_to_all | solution.py:274
  10.3 0.0 copy-start.4
  10.3 0.0 copy-start.5
  10.3 0.0 copy-done.3
  10.3 0.7 copy-done.4
  11.0 0.0 copy-done.5
  11.0 0.0 copy-start
  11.0 0.0 copy-start.1
  11.0 0.3 mix_kernel.1._.mix_ref
  11.3 5.5 %all-to-all-done = f32[8,64,128]{2,1,0:T(8,128)S(1)} async-done(((f32[8,64,128]{2,1,0:T(8,128)}), f32[8,64,128]{2,1,0:T(8,128)S(1)}, u32[]{:S(2)}, u32[]{:S(2)}) %all-to-all-start) | async-done | bytes 262176 | tf_op jit(solution)/shard_map/all_to_all | solution.py:274
  16.8 0.0 copy-done
  16.8 0.0 copy-done.1
  16.8 0.7 terms_kernel.1
  17.5 8.3 %all_to_all.43 = f32[8,16,128]{2,1,0:T(8,128)S(1)} all-to-all(f32[8,16,128]{2,1,0:T(8,128)S(1)} %bitcast.20), channel_id=1, replica_groups=mesh['grid'=64,'member'=8] {'member'}, dimensions={0} | all-to-all | bytes 131072 | tf_op jit(solution)/shard_map/all_to_all | solution.py:274
  25.7 0.1 window_kernel.1
  25.8 0.0 copy-start.2
  25.8 28.1 %all_to_all.44 = f32[64,4,128]{2,1,0:T(4,128)S(1)} all-to-all(f32[64,4,128]{2,1,0:T(4,128)S(1)} %bitcast.17), channel_id=1, replica_groups=mesh['grid'=64,'member'=8] {'grid'}, dimensions={0} | all-to-all | bytes 262144 | tf_op jit(solution)/shard_map/all_to_all | solution.py:274
  53.9 0.0 copy-done.2
  53.9 0.4 combine_kernel.1
  54.3 10.5 %all_to_all.45 = f32[8,24,128]{2,1,0:T(8,128)S(1)} all-to-all(f32[8,24,128]{2,1,0:T(8,128)S(1)} %bitcast.19), channel_id=1, replica_groups=mesh['grid'=64,'member'=8] {'member'}, dimensions={0} | all-to-all | bytes 196608 | tf_op jit(solution)/shard_map/all_to_all | solution.py:274
  64.8 3.1 %transform_kernel.1 = f32[64,128]{1,0:T(8,128)S(1)} custom-call(f32[192,128]{1,0:T(8,128)S(1)} %bitcast.18), custom_call_target="tpu_custom_call" | custom-call | tf_op jit(solution)/shard_map/transform_kernel/pallas_call | solution.py:65
  67.9 7.9 %all_to_all.46 = f32[16,4,128]{2,1,0:T(4,128)S(1)} all-to-all(f32[16,4,128]{2,1,0:T(4,128)S(1)} %bitcast.22), channel_id=1, replica_groups=mesh['grid'=64,'member'=8] {'member'}, dimensions={0} | all-to-all | bytes 65536 | tf_op jit(solution)/shard_map/all_to_all | solution.py:274
  75.8 0.6 copy.9
Async XLA Ops:
  0.0 10.3 %copy-start.3 = (f32[16,8,8]{0,2,1:T(8,128)S(1)}, f32[16,8,8]{0,2,1:T(8,128)}, u32[]{:S(2)}) copy-start(f32[16,8,8]{0,2,1:T(8,128)} %param.11) | copy-start | bytes 12292
  0.0 16.8 %all-to-all-start = ((f32[8,64,128]{2,1,0:T(8,128)}), f32[8,64,128]{2,1,0:T(8,128)S(1)}, u32[]{:S(2)}, u32[]{:S(2)}) async-start(f32[8,64,128]{2,1,0:T(8,128)} %bitcast.27), calls=%async_computation | async-start | bytes 524288 | tf_op jit(solution)/shard_map/all_to_all | solution.py:274
  10.3 0.7 copy-start.4
  10.3 0.7 copy-start.5
  11.0 5.8 %copy-start = (f32[128,128]{1,0:T(8,128)S(1)}, f32[128,128]{1,0:T(8,128)}, u32[]{:S(2)}) copy-start(f32[128,128]{1,0:T(8,128)} %value_ref.1) | copy-start | bytes 196612
  11.0 5.8 %copy-start.1 = (f32[128,128]{1,0:T(8,128)S(1)}, f32[128,128]{1,0:T(8,128)}, u32[]{:S(2)}) copy-start(f32[128,128]{1,0:T(8,128)} %rinv_ref.1) | copy-start | bytes 196612
  25.8 28.1 %copy-start.2 = (f32[16,4,128]{2,1,0:T(4,128)S(1)}, f32[16,4,128]{2,1,0:T(4,128)}, u32[]{:S(2)}) copy-start(f32[16,4,128]{2,1,0:T(4,128)} %param.7) | copy-start | bytes 98308

commit v5 on v4

--- a/solution.py
+++ b/solution.py
@@ -49,7 +49,7 @@
     return lax.dot_general(left, right, (((1,), (1,)), ((), ())), preferred_element_type=F32)
 
 
-def product(left, right, form, axis):
+def product(left, right, form=dot, axis=0):
     high, middle, low = left
     first, second, third = right
     both = jnp.concatenate([high, middle], axis=1)
@@ -247,21 +247,28 @@
     for step in range(NS - 1):
         blocks = [spread(root[g], ones) for g in groups]
         if step == 0:
-            square = [product(thirds(root[g]), blocks[g], dot, 0) for g in groups]
+            square = [product(thirds(root[g]), blocks[g]) for g in groups]
         else:
-            square = [product(thirds(root[g]), blocks[g], dot, 0) for g in groups]
-            inverse = [1.5 * inverse[g] - 0.5 * product(thirds(inverse[g]), blocks[g], dot, 0) for g in groups]
+            square = [product(thirds(root[g]), blocks[g]) for g in groups]
         middle = [2.25 * identity - 1.5 * root[g] + 0.25 * square[g] for g in groups]
-        root = [product(thirds(middle[g]), blocks[g], dot, 0) for g in groups]
+        if step == 0:
+            root = [product(thirds(middle[g]), blocks[g]) for g in groups]
+        else:
+            both = [
+                product(thirds(jnp.concatenate([middle[g], inverse[g]], axis=0)), blocks[g])
+                for g in groups
+            ]
+            root = [both[g][:K] for g in groups]
+            inverse = [1.5 * inverse[g] - 0.5 * both[g][K:] for g in groups]
     blocks = [spread(root[g], ones) for g in groups]
-    inverse = [1.5 * inverse[g] - 0.5 * product(thirds(inverse[g]), blocks[g], dot, 0) for g in groups]
+    inverse = [1.5 * inverse[g] - 0.5 * product(thirds(inverse[g]), blocks[g]) for g in groups]
     for s0 in range(2):
         both = slice(2 * s0, 2 * s0 + 2)
         wide = jnp.concatenate(inverse[both], axis=1)
         state = jnp.concatenate(
             [in_ref[pl.ds(16 + s0 * 4 + kk, 8, stride=24), :] for kk in range(4)], axis=0
         )
-        moved = product(thirds(wide), spread(state, point), dot, 0)
+        moved = product(thirds(wide), spread(state, point))
         first = segment_sum(wide * jnp.concatenate(drives[both], axis=1), point)
         norm = jnp.sqrt(segment_sum(jnp.concatenate(squares[both], axis=1), point)[:1])
         shift = jnp.sum(first * moved, axis=0, keepdims=True) / norm

time: 76.9 us -> 76.6 us (level)
  no operation moved by 1% of the time
where the time goes in v5:
time: 76.6 us; the launch traced here: 76.2 us
  blocking collectives  54.7 us (71%)
  starting transfers between devices  10.3 us (13%)
  waiting for transfers between devices  5.47 us (7%)
  Pallas kernels  4.39 us (6%)
  local copies, waits for them, and re-layouts  1.31 us (2%)
    all_to_all x4, blocking collectives, swap(): return lax.all_to_all(array, axis, split_axis=0, concat_axis=0, tiled=True)  54.7 us
    all_to_all x1, starting transfers between devices, swap(): return lax.all_to_all(array, axis, split_axis=0, concat_axis=0, tiled=True)  10.3 us
    all_to_all x1, waiting for transfers between devices, swap(): return lax.all_to_all(array, axis, split_axis=0, concat_axis=0, tiled=True)  5.47 us
    pallas_call x5, Pallas kernels, call(): pl.pallas_call(kernel, out_shape=[out if isinstance(out, jax.ShapeDtypeSt...  4.39 us
  transfers between devices with their start and end apart: 1, of which 1 were waited for; matrix products, arithmetic and copies ran while one was open for 0% of the time, Pallas kernels for 0%

profile of v5, /device:TPU:1, one launch (start us, length us, event | category | flops | bytes accessed | tf_op | source)
XLA Modules:
  0.0 76.2 jit_solution(6486307149875887926)
XLA Ops:
  0.0 0.0 copy-start.3
  0.0 10.3 %all-to-all-start = ((f32[8,64,128]{2,1,0:T(8,128)}), f32[8,64,128]{2,1,0:T(8,128)S(1)}, u32[]{:S(2)}, u32[]{:S(2)}) async-start(f32[8,64,128]{2,1,0:T(8,128)} %bitcast.27), calls=%async_computation | async-start | bytes 524288 | tf_op jit(solution)/shard_map/all_to_all | solution.py:281
  10.3 0.0 copy-start.4
  10.3 0.0 copy-start.5
  10.3 0.0 copy-done.3
  10.3 0.7 copy-done.4
  11.0 0.0 copy-done.5
  11.0 0.0 copy-start
  11.0 0.0 copy-start.1
  11.0 0.3 mix_kernel.1._.mix_ref
  11.3 5.5 %all-to-all-done = f32[8,64,128]{2,1,0:T(8,128)S(1)} async-done(((f32[8,64,128]{2,1,0:T(8,128)}), f32[8,64,128]{2,1,0:T(8,128)S(1)}, u32[]{:S(2)}, u32[]{:S(2)}) %all-to-all-start) | async-done | bytes 262176 | tf_op jit(solution)/shard_map/all_to_all | solution.py:281
  16.8 0.0 copy-done
  16.8 0.0 copy-done.1
  16.8 0.7 terms_kernel.1
  17.5 8.3 %all_to_all.43 = f32[8,16,128]{2,1,0:T(8,128)S(1)} all-to-all(f32[8,16,128]{2,1,0:T(8,128)S(1)} %bitcast.20), channel_id=1, replica_groups=mesh['grid'=64,'member'=8] {'member'}, dimensions={0} | all-to-all | bytes 131072 | tf_op jit(solution)/shard_map/all_to_all | solution.py:281
  25.7 0.1 window_kernel.1
  25.8 0.0 copy-start.2
  25.8 28.1 %all_to_all.44 = f32[64,4,128]{2,1,0:T(4,128)S(1)} all-to-all(f32[64,4,128]{2,1,0:T(4,128)S(1)} %bitcast.17), channel_id=1, replica_groups=mesh['grid'=64,'member'=8] {'grid'}, dimensions={0} | all-to-all | bytes 262144 | tf_op jit(solution)/shard_map/all_to_all | solution.py:281
  53.9 0.0 copy-done.2
  53.9 0.4 combine_kernel.1
  54.3 10.5 %all_to_all.45 = f32[8,24,128]{2,1,0:T(8,128)S(1)} all-to-all(f32[8,24,128]{2,1,0:T(8,128)S(1)} %bitcast.19), channel_id=1, replica_groups=mesh['grid'=64,'member'=8] {'member'}, dimensions={0} | all-to-all | bytes 196608 | tf_op jit(solution)/shard_map/all_to_all | solution.py:281
  64.8 2.9 %transform_kernel.1 = f32[64,128]{1,0:T(8,128)S(1)} custom-call(f32[192,128]{1,0:T(8,128)S(1)} %bitcast.18), custom_call_target="tpu_custom_call" | custom-call | tf_op jit(solution)/shard_map/transform_kernel/pallas_call | solution.py:65
  67.7 7.9 %all_to_all.46 = f32[16,4,128]{2,1,0:T(4,128)S(1)} all-to-all(f32[16,4,128]{2,1,0:T(4,128)S(1)} %bitcast.22), channel_id=1, replica_groups=mesh['grid'=64,'member'=8] {'member'}, dimensions={0} | all-to-all | bytes 65536 | tf_op jit(solution)/shard_map/all_to_all | solution.py:281
  75.6 0.6 copy.9
Async XLA Ops:
  0.0 10.3 %copy-start.3 = (f32[16,8,8]{0,2,1:T(8,128)S(1)}, f32[16,8,8]{0,2,1:T(8,128)}, u32[]{:S(2)}) copy-start(f32[16,8,8]{0,2,1:T(8,128)} %param.11) | copy-start | bytes 12292
  0.0 16.8 %all-to-all-start = ((f32[8,64,128]{2,1,0:T(8,128)}), f32[8,64,128]{2,1,0:T(8,128)S(1)}, u32[]{:S(2)}, u32[]{:S(2)}) async-start(f32[8,64,128]{2,1,0:T(8,128)} %bitcast.27), calls=%async_computation | async-start | bytes 524288 | tf_op jit(solution)/shard_map/all_to_all | solution.py:281
  10.3 0.7 copy-start.4
  10.3 0.7 copy-start.5
  11.0 5.8 %copy-start = (f32[128,128]{1,0:T(8,128)S(1)}, f32[128,128]{1,0:T(8,128)}, u32[]{:S(2)}) copy-start(f32[128,128]{1,0:T(8,128)} %value_ref.1) | copy-start | bytes 196612
  11.0 5.8 %copy-start.1 = (f32[128,128]{1,0:T(8,128)S(1)}, f32[128,128]{1,0:T(8,128)}, u32[]{:S(2)}) copy-start(f32[128,128]{1,0:T(8,128)} %rinv_ref.1) | copy-start | bytes 196612
  25.8 28.1 %copy-start.2 = (f32[16,4,128]{2,1,0:T(4,128)S(1)}, f32[16,4,128]{2,1,0:T(4,128)}, u32[]{:S(2)}) copy-start(f32[16,4,128]{2,1,0:T(4,128)} %param.7) | copy-start | bytes 98308

commit v6 on v5

--- a/solution.py
+++ b/solution.py
@@ -52,6 +52,11 @@
 def product(left, right, form=dot, axis=0):
     high, middle, low = left
     first, second, third = right
+    if axis:
+        return form(
+            jnp.concatenate([high, low, middle, middle, high, high], axis=1),
+            jnp.concatenate([third, first, second, first, second, first], axis=1),
+        )
     both = jnp.concatenate([high, middle], axis=1)
     return (
         form(both, jnp.concatenate([first] * 2, axis=axis))
@@ -193,13 +198,6 @@
     return wide[:rows] + wide[rows : 2 * rows] + wide[2 * rows :]
 
 
-def mirrored(value, identity, ones):
-    high, middle, low = [jnp.concatenate([third] * 4, axis=0) * ones for third in thirds(value)]
-    return dot_rows(
-        jnp.concatenate([identity] * 2, axis=1), jnp.concatenate([high, middle], axis=1)
-    ) + dot_rows(identity, low)
-
-
 def transform_kernel(in_ref, out_ref):
     def same(shape, rows, lanes):
         return (iota(shape, 0) // rows == iota(shape, 1) // lanes).astype(F32).astype(BF16)
@@ -231,7 +229,8 @@
                 acc = jnp.where(inside, tile, acc)
             rows.append(acc)
         packed = jnp.concatenate(rows, axis=0)
-        flipped = mirrored(packed, identity.astype(BF16), ones)
+        upright = jnp.transpose(packed)
+        flipped = jnp.concatenate([upright[q * K : q * K + K] for q in range(4)], axis=1)
         amats.append(jnp.where(keep, packed, flipped) + (K - 1.0) * identity)
         square = packed + (K - 1.0) * identity
         square = jnp.sum(square * square * times, axis=0, keepdims=True)
@@ -244,15 +243,16 @@
     frobenius = [jnp.sqrt(sums[8 * g : 8 * g + 1]) for g in groups]
     root = [amats[g] / frobenius[g] for g in groups]
     inverse = [1.5 * identity - 0.5 * root[g] for g in groups]
+    blocks = [spread(amats[g], ones) for g in groups]
     for step in range(NS - 1):
-        blocks = [spread(root[g], ones) for g in groups]
         if step == 0:
-            square = [product(thirds(root[g]), blocks[g]) for g in groups]
+            square = [product(thirds(amats[g]), blocks[g]) / sums[8 * g : 8 * g + 1] for g in groups]
         else:
+            blocks = [spread(root[g], ones) for g in groups]
             square = [product(thirds(root[g]), blocks[g]) for g in groups]
         middle = [2.25 * identity - 1.5 * root[g] + 0.25 * square[g] for g in groups]
         if step == 0:
-            root = [product(thirds(middle[g]), blocks[g]) for g in groups]
+            root = [product(thirds(middle[g]), blocks[g]) / frobenius[g] for g in groups]
         else:
             both = [
                 product(thirds(jnp.concatenate([middle[g], inverse[g]], axis=0)), blocks[g])

time: 76.6 us -> 76.6 us (level)
  no operation moved by 1% of the time
where the time goes in v6:
time: 76.6 us; the launch traced here: 76.1 us
  blocking collectives  54.7 us (71%)
  starting transfers between devices  10.3 us (13%)
  waiting for transfers between devices  5.47 us (7%)
  Pallas kernels  4.31 us (6%)
  local copies, waits for them, and re-layouts  1.31 us (2%)
    all_to_all x4, blocking collectives, swap(): return lax.all_to_all(array, axis, split_axis=0, concat_axis=0, tiled=True)  54.7 us
    all_to_all x1, starting transfers between devices, swap(): return lax.all_to_all(array, axis, split_axis=0, concat_axis=0, tiled=True)  10.3 us
    all_to_all x1, waiting for transfers between devices, swap(): return lax.all_to_all(array, axis, split_axis=0, concat_axis=0, tiled=True)  5.47 us
    pallas_call x5, Pallas kernels, call(): pl.pallas_call(kernel, out_shape=[out if isinstance(out, jax.ShapeDtypeSt...  4.31 us
  transfers between devices with their start and end apart: 1, of which 1 were waited for; matrix products, arithmetic and copies ran while one was open for 0% of the time, Pallas kernels for 0%

profile of v6, /device:TPU:1, one launch (start us, length us, event | category | flops | bytes accessed | tf_op | source)
XLA Modules:
  0.0 76.1 jit_solution(14902097747189936406)
XLA Ops:
  0.0 0.0 copy-start.3
  0.0 10.3 %all-to-all-start = ((f32[8,64,128]{2,1,0:T(8,128)}), f32[8,64,128]{2,1,0:T(8,128)S(1)}, u32[]{:S(2)}, u32[]{:S(2)}) async-start(f32[8,64,128]{2,1,0:T(8,128)} %bitcast.27), calls=%async_computation | async-start | bytes 524288 | tf_op jit(solution)/shard_map/all_to_all | solution.py:281
  10.3 0.0 copy-start.4
  10.3 0.0 copy-start.5
  10.3 0.0 copy-done.3
  10.3 0.7 copy-done.4
  11.0 0.0 copy-done.5
  11.0 0.0 copy-start
  11.0 0.0 copy-start.1
  11.0 0.3 mix_kernel.1._.mix_ref
  11.3 5.5 %all-to-all-done = f32[8,64,128]{2,1,0:T(8,128)S(1)} async-done(((f32[8,64,128]{2,1,0:T(8,128)}), f32[8,64,128]{2,1,0:T(8,128)S(1)}, u32[]{:S(2)}, u32[]{:S(2)}) %all-to-all-start) | async-done | bytes 262176 | tf_op jit(solution)/shard_map/all_to_all | solution.py:281
  16.8 0.0 copy-done
  16.8 0.0 copy-done.1
  16.8 0.7 terms_kernel.1
  17.4 8.3 %all_to_all.43 = f32[8,16,128]{2,1,0:T(8,128)S(1)} all-to-all(f32[8,16,128]{2,1,0:T(8,128)S(1)} %bitcast.20), channel_id=1, replica_groups=mesh['grid'=64,'member'=8] {'member'}, dimensions={0} | all-to-all | bytes 131072 | tf_op jit(solution)/shard_map/all_to_all | solution.py:281
  25.7 0.1 window_kernel.1
  25.8 0.0 copy-start.2
  25.8 28.1 %all_to_all.44 = f32[64,4,128]{2,1,0:T(4,128)S(1)} all-to-all(f32[64,4,128]{2,1,0:T(4,128)S(1)} %bitcast.17), channel_id=1, replica_groups=mesh['grid'=64,'member'=8] {'grid'}, dimensions={0} | all-to-all | bytes 262144 | tf_op jit(solution)/shard_map/all_to_all | solution.py:281
  53.9 0.0 copy-done.2
  53.9 0.4 combine_kernel.1
  54.3 10.5 %all_to_all.45 = f32[8,24,128]{2,1,0:T(8,128)S(1)} all-to-all(f32[8,24,128]{2,1,0:T(8,128)S(1)} %bitcast.19), channel_id=1, replica_groups=mesh['grid'=64,'member'=8] {'member'}, dimensions={0} | all-to-all | bytes 196608 | tf_op jit(solution)/shard_map/all_to_all | solution.py:281
  64.8 2.8 %transform_kernel.1 = f32[64,128]{1,0:T(8,128)S(1)} custom-call(f32[192,128]{1,0:T(8,128)S(1)} %bitcast.18), custom_call_target="tpu_custom_call" | custom-call | tf_op jit(solution)/shard_map/transform_kernel/pallas_call | solution.py:70
  67.6 7.9 %all_to_all.46 = f32[16,4,128]{2,1,0:T(4,128)S(1)} all-to-all(f32[16,4,128]{2,1,0:T(4,128)S(1)} %bitcast.22), channel_id=1, replica_groups=mesh['grid'=64,'member'=8] {'member'}, dimensions={0} | all-to-all | bytes 65536 | tf_op jit(solution)/shard_map/all_to_all | solution.py:281
  75.5 0.6 copy.9
Async XLA Ops:
  0.0 10.3 %copy-start.3 = (f32[16,8,8]{0,2,1:T(8,128)S(1)}, f32[16,8,8]{0,2,1:T(8,128)}, u32[]{:S(2)}) copy-start(f32[16,8,8]{0,2,1:T(8,128)} %param.11) | copy-start | bytes 12292
  0.0 16.8 %all-to-all-start = ((f32[8,64,128]{2,1,0:T(8,128)}), f32[8,64,128]{2,1,0:T(8,128)S(1)}, u32[]{:S(2)}, u32[]{:S(2)}) async-start(f32[8,64,128]{2,1,0:T(8,128)} %bitcast.27), calls=%async_computation | async-start | bytes 524288 | tf_op jit(solution)/shard_map/all_to_all | solution.py:281
  10.3 0.7 copy-start.4
  10.3 0.7 copy-start.5
  11.0 5.8 %copy-start = (f32[128,128]{1,0:T(8,128)S(1)}, f32[128,128]{1,0:T(8,128)}, u32[]{:S(2)}) copy-start(f32[128,128]{1,0:T(8,128)} %value_ref.1) | copy-start | bytes 196612
  11.0 5.8 %copy-start.1 = (f32[128,128]{1,0:T(8,128)S(1)}, f32[128,128]{1,0:T(8,128)}, u32[]{:S(2)}) copy-start(f32[128,128]{1,0:T(8,128)} %rinv_ref.1) | copy-start | bytes 196612
  25.8 28.1 %copy-start.2 = (f32[16,4,128]{2,1,0:T(4,128)S(1)}, f32[16,4,128]{2,1,0:T(4,128)}, u32[]{:S(2)}) copy-start(f32[16,4,128]{2,1,0:T(4,128)} %param.7) | copy-start | bytes 98308

commit v7 on v5

--- a/solution.py
+++ b/solution.py
@@ -300,7 +300,7 @@
     )
     shares = swap(terms, "member")
     (windows,) = call(window_kernel, (4 * GRID,), shares)
-    arrived = swap(windows.reshape(GRID, 4, LANES), "grid").reshape(4 * GRID, LANES)
+    arrived = swap(windows.reshape(GRID, 1, 4 * LANES), "grid").reshape(4 * GRID, LANES)
     (combos,) = call(
         combine_kernel,
         (8 * 24,),

time: 76.6 us -> 76.6 us (level)
  no operation moved by 1% of the time
where the time goes in v7:
time: 76.6 us; the launch traced here: 76.2 us
  blocking collectives  54.7 us (71%)
  starting transfers between devices  10.3 us (13%)
  waiting for transfers between devices  5.47 us (7%)
  Pallas kernels  4.39 us (6%)
  local copies, waits for them, and re-layouts  1.31 us (2%)
    all_to_all x4, blocking collectives, swap(): return lax.all_to_all(array, axis, split_axis=0, concat_axis=0, tiled=True)  54.7 us
    all_to_all x1, starting transfers between devices, swap(): return lax.all_to_all(array, axis, split_axis=0, concat_axis=0, tiled=True)  10.3 us
    all_to_all x1, waiting for transfers between devices, swap(): return lax.all_to_all(array, axis, split_axis=0, concat_axis=0, tiled=True)  5.47 us
    pallas_call x5, Pallas kernels, call(): pl.pallas_call(kernel, out_shape=[out if isinstance(out, jax.ShapeDtypeSt...  4.39 us
  transfers between devices with their start and end apart: 1, of which 1 were waited for; matrix products, arithmetic and copies ran while one was open for 0% of the time, Pallas kernels for 0%

profile of v7, /device:TPU:1, one launch (start us, length us, event | category | flops | bytes accessed | tf_op | source)
XLA Modules:
  0.0 76.2 jit_solution(6486307149875887926)
XLA Ops:
  0.0 0.0 copy-start.3
  0.0 10.3 %all-to-all-start = ((f32[8,64,128]{2,1,0:T(8,128)}), f32[8,64,128]{2,1,0:T(8,128)S(1)}, u32[]{:S(2)}, u32[]{:S(2)}) async-start(f32[8,64,128]{2,1,0:T(8,128)} %bitcast.27), calls=%async_computation | async-start | bytes 524288 | tf_op jit(solution)/shard_map/all_to_all | solution.py:281
  10.3 0.0 copy-start.4
  10.3 0.0 copy-start.5
  10.3 0.0 copy-done.3
  10.3 0.7 copy-done.4
  11.0 0.0 copy-done.5
  11.0 0.0 copy-start
  11.0 0.0 copy-start.1
  11.0 0.3 mix_kernel.1._.mix_ref
  11.3 5.5 %all-to-all-done = f32[8,64,128]{2,1,0:T(8,128)S(1)} async-done(((f32[8,64,128]{2,1,0:T(8,128)}), f32[8,64,128]{2,1,0:T(8,128)S(1)}, u32[]{:S(2)}, u32[]{:S(2)}) %all-to-all-start) | async-done | bytes 262176 | tf_op jit(solution)/shard_map/all_to_all | solution.py:281
  16.8 0.0 copy-done
  16.8 0.0 copy-done.1
  16.8 0.7 terms_kernel.1
  17.5 8.3 %all_to_all.43 = f32[8,16,128]{2,1,0:T(8,128)S(1)} all-to-all(f32[8,16,128]{2,1,0:T(8,128)S(1)} %bitcast.20), channel_id=1, replica_groups=mesh['grid'=64,'member'=8] {'member'}, dimensions={0} | all-to-all | bytes 131072 | tf_op jit(solution)/shard_map/all_to_all | solution.py:281
  25.7 0.1 window_kernel.1
  25.8 0.0 copy-start.2
  25.8 28.1 %all_to_all.44 = f32[64,1,512]{2,1,0:T(1,128)S(1)} all-to-all(f32[64,1,512]{2,1,0:T(1,128)S(1)} %bitcast.17), channel_id=1, replica_groups=mesh['grid'=64,'member'=8] {'grid'}, dimensions={0} | all-to-all | bytes 262144 | tf_op jit(solution)/shard_map/all_to_all | solution.py:281
  53.9 0.0 copy-done.2
  53.9 0.4 combine_kernel.1
  54.3 10.5 %all_to_all.45 = f32[8,24,128]{2,1,0:T(8,128)S(1)} all-to-all(f32[8,24,128]{2,1,0:T(8,128)S(1)} %bitcast.19), channel_id=1, replica_groups=mesh['grid'=64,'member'=8] {'member'}, dimensions={0} | all-to-all | bytes 196608 | tf_op jit(solution)/shard_map/all_to_all | solution.py:281
  64.8 2.9 %transform_kernel.1 = f32[64,128]{1,0:T(8,128)S(1)} custom-call(f32[192,128]{1,0:T(8,128)S(1)} %bitcast.18), custom_call_target="tpu_custom_call" | custom-call | tf_op jit(solution)/shard_map/transform_kernel/pallas_call | solution.py:65
  67.7 7.9 %all_to_all.46 = f32[16,4,128]{2,1,0:T(4,128)S(1)} all-to-all(f32[16,4,128]{2,1,0:T(4,128)S(1)} %bitcast.22), channel_id=1, replica_groups=mesh['grid'=64,'member'=8] {'member'}, dimensions={0} | all-to-all | bytes 65536 | tf_op jit(solution)/shard_map/all_to_all | solution.py:281
  75.6 0.6 copy.10
Async XLA Ops:
  0.0 10.3 %copy-start.3 = (f32[16,8,8]{0,2,1:T(8,128)S(1)}, f32[16,8,8]{0,2,1:T(8,128)}, u32[]{:S(2)}) copy-start(f32[16,8,8]{0,2,1:T(8,128)} %param.11) | copy-start | bytes 12292
  0.0 16.8 %all-to-all-start = ((f32[8,64,128]{2,1,0:T(8,128)}), f32[8,64,128]{2,1,0:T(8,128)S(1)}, u32[]{:S(2)}, u32[]{:S(2)}) async-start(f32[8,64,128]{2,1,0:T(8,128)} %bitcast.27), calls=%async_computation | async-start | bytes 524288 | tf_op jit(solution)/shard_map/all_to_all | solution.py:281
  10.3 0.7 copy-start.4
  10.3 0.7 copy-start.5
  11.0 5.8 %copy-start = (f32[128,128]{1,0:T(8,128)S(1)}, f32[128,128]{1,0:T(8,128)}, u32[]{:S(2)}) copy-start(f32[128,128]{1,0:T(8,128)} %value_ref.1) | copy-start | bytes 196612
  11.0 5.8 %copy-start.1 = (f32[128,128]{1,0:T(8,128)S(1)}, f32[128,128]{1,0:T(8,128)}, u32[]{:S(2)}) copy-start(f32[128,128]{1,0:T(8,128)} %rinv_ref.1) | copy-start | bytes 196612
  25.8 28.1 %copy-start.2 = (f32[16,4,128]{2,1,0:T(4,128)S(1)}, f32[16,4,128]{2,1,0:T(4,128)}, u32[]{:S(2)}) copy-start(f32[16,4,128]{2,1,0:T(4,128)} %param.7) | copy-start | bytes 98308
